TPU v7x, 32 devices: a whole 2x2x4 slice. The times are simulated.
32 devices in a mesh: batch: 4 (over z), seq: 8 (over y, x, core).
Axes of the slice: x: 2, y: 2, z: 4, core: 2. Of those that a mesh axis runs over, the one named last changes fastest.
Arguments:
- tokens: bfloat16 [16, 2048, 768], P('batch', 'seq'), may hold values from -6 to 6
- segment_ids: int32 [16, 2048], P('batch', 'seq'), may hold values from -1 to 5, as said below
- attn_gain: bfloat16 [768], replicated, may hold values from 0.5 to 1.5
- attn_shift: bfloat16 [768], replicated, may hold values from -1.75 to 1.75
- mlp_gain: bfloat16 [768], replicated, may hold values from 0.5 to 1.5
- mlp_shift: bfloat16 [768], replicated, may hold values from -1.75 to 1.75
- w_query: bfloat16 [768, 768], replicated, may hold values from -0.21875 to 0.21875
- b_query: bfloat16 [768], replicated, may hold values from -1.75 to 1.75
- w_keyvalue: bfloat16 [768, 128], replicated, may hold values from -0.21875 to 0.21875
- w_out: bfloat16 [768, 768], replicated, may hold values from -1.75 to 1.75
- b_out: bfloat16 [768], replicated, may hold values from -1.75 to 1.75
- w_up: bfloat16 [768, 3072], replicated, may hold values from -0.21875 to 0.21875
- b_up: bfloat16 [3072], replicated, may hold values from -1.75 to 1.75
- w_down: bfloat16 [3072, 768], replicated, may hold values from -0.109375 to 0.109375
- b_down: bfloat16 [768], replicated, may hold values from -1.75 to 1.75
- out_grad: bfloat16 [16, 2048, 768], P('batch', 'seq'), may hold values from -6 to 6
Outputs:
- output: bfloat16 [16, 2048, 768], P('batch', 'seq')
- keyvalue: bfloat16 [16, 2048, 128], P('batch', 'seq')
- tokens_grad: bfloat16 [16, 2048, 768], P('batch', 'seq')
- attn_gain_grad: float32 [768], P(('batch', 'seq'))
- attn_shift_grad: float32 [768], P(('batch', 'seq'))
- mlp_gain_grad: float32 [768], P(('batch', 'seq'))
- mlp_shift_grad: float32 [768], P(('batch', 'seq'))
- w_query_grad: float32 [768, 768], P(('batch', 'seq'))
- b_query_grad: float32 [768], P(('batch', 'seq'))
- w_keyvalue_grad: float32 [768, 128], P(('batch', 'seq'))
- w_out_grad: float32 [768, 768], P(None, ('batch', 'seq'))
- b_out_grad: float32 [768], P(('batch', 'seq'))
- w_up_grad: float32 [768, 3072], P(('batch', 'seq'))
- b_up_grad: float32 [3072], P(('batch', 'seq'))
- w_down_grad: float32 [3072, 768], P(None, ('batch', 'seq'))
- b_down_grad: float32 [768], P(('batch', 'seq'))
Inputs may be any that keep to these rules, and one draw needn't show every extreme that they name: `segment_ids`: each row holds 6 documents with ids 0 to 5 in order, each a nonempty run of positions, followed by one or more padding positions with id -1 at the row's end.
All inputs are finite; a program needn't handle non-finite values.
Results may differ from a plain program's by a relative error of at most 0.011.
Values may be sent and summed in bfloat16 or wider, within the bound.
No kernel may reach another device: no remote copies, remote signals or barrier semaphores. Data moves between devices by JAX's collectives and lax.ppermute only.
A program may use at most 256 MiB of HBM per device.

v0:
```python
import functools
import math

import jax
import jax.numpy as jnp
from jax import lax
from jax.experimental import pallas as pl
from jax.experimental.pallas import tpu as pltpu
from jax.sharding import PartitionSpec as P

ROT_DIMS = 16
HALF_ROT = ROT_DIMS // 2
DOCS = 6
EPSILON = 1e-05
KEY_BLOCK = 256
COUNT_ROWS = 16
LANES = 128
NEGATIVE = -1e30
BF = jnp.bfloat16
F32 = jnp.float32
NN = (((1,), (0,)), ((), ()))
NT = (((1,), (1,)), ((), ()))
TN = (((0,), (0,)), ((), ()))


def matmul(left, right, dims=NN):
    return lax.dot_general(left, right, dims, preferred_element_type=F32)


def params(limit):
    return pltpu.CompilerParams(
        dimension_semantics=("arbitrary",), vmem_limit_bytes=limit * 1024 * 1024
    )


LONG = pl.CostEstimate(flops=4 * 10**10, transcendentals=0, bytes_accessed=10**7)

LONGEST = pl.CostEstimate(flops=3 * 10**11, transcendentals=0, bytes_accessed=10**7)


def short(size):
    return pl.CostEstimate(flops=0, transcendentals=0, bytes_accessed=size)


def whole(shape):
    return pl.BlockSpec(shape, lambda *_: (0,) * len(shape))


def permute_rows(values, order, rows):
    return jnp.concatenate([values[b * rows : (b + 1) * rows] for b in order], axis=0)


def row_of(ref):
    return ref[...].astype(F32).reshape(1, ref.shape[0])


def valid_column(segment_row):
    length = segment_row.shape[-1]
    row = jnp.broadcast_to((segment_row >= 0).astype(F32), (LANES, length))
    return row.T[:, :1]


def norm_parts(values):
    center = values - jnp.mean(values, axis=-1, keepdims=True)
    spread = jnp.mean(center * center, axis=-1, keepdims=True)
    scale = lax.rsqrt(spread + EPSILON)
    return center * scale, scale


def turn(values, cosine, sine):
    leading = values[:HALF_ROT]
    trailing = values[HALF_ROT:ROT_DIMS]
    return jnp.concatenate(
        [leading * cosine - trailing * sine, trailing * cosine + leading * sine, values[ROT_DIMS:]],
        axis=0,
    )


def entry_kernel(
    head_size, order_a, order_b, rows, permuted,
    tok_ref, og_ref, seg_ref, ag_ref, as_ref, mg_ref, ms_ref, bq_ref, wq_ref, wkv_ref, wo_ref,
    cos_ref, sin_ref, mlp_ref, bg_ref, mlp_t_ref, bg_t_ref, attn_t_ref, q_t_ref, g_t_ref, kv_ref, pay_ref,
):
    x = tok_ref[0].astype(F32)
    length, width = x.shape
    n, _ = norm_parts(x)
    attn_in = (n * row_of(ag_ref) + row_of(as_ref)).astype(BF)
    mlp_in = (n * row_of(mg_ref) + row_of(ms_ref)).astype(BF)
    segments = seg_ref[pl.ds(pl.program_id(0), 1), :]
    bg = (og_ref[0].astype(F32) * valid_column(segments)).astype(BF)
    mlp_ref[...] = mlp_in
    bg_ref[...] = bg

    def turned(values, order):
        flipped = values.astype(F32).T
        if permuted:
            flipped = permute_rows(flipped, order, rows)
        return flipped.astype(BF)

    mlp_t_ref[...] = turned(mlp_in, order_a)
    attn_t_ref[...] = turned(attn_in, order_a)
    bg_t_ref[...] = turned(bg, order_b)

    cosine, sine = cos_ref[...], sin_ref[...]
    score_scale = 1.0 / math.sqrt(head_size)
    query_t = (matmul(attn_in, wq_ref[...]) + row_of(bq_ref)).T
    grad_t = matmul(wo_ref[...], bg, NT)
    for h in range(width // head_size):
        part = query_t[h * head_size : (h + 1) * head_size]
        q_t_ref[0, :, h * length : (h + 1) * length] = (
            turn(part, cosine, sine) * score_scale
        ).astype(BF)
        g_t_ref[0, :, h * length : (h + 1) * length] = grad_t[
            h * head_size : (h + 1) * head_size
        ].astype(BF)
    kv_t = matmul(attn_in, wkv_ref[...]).T
    kv = turn(kv_t, cosine, sine).T.astype(BF)
    kv_ref[0] = kv
    pay_ref[0, :length] = kv
    lane = lax.broadcasted_iota(jnp.int32, (1, LANES), 1)
    counts = jnp.zeros((1, LANES), F32)
    for c in range(DOCS):
        total = jnp.sum((segments == c).astype(F32), axis=1, keepdims=True)
        counts = counts + jnp.where(lane == c, total, 0.0)
    pay_ref[0, length:] = jnp.broadcast_to(counts, (COUNT_ROWS, LANES)).astype(BF)


def gelu_parts(hidden):
    cdf = 0.5 * (1.0 + lax.erf(hidden * math.sqrt(0.5)))
    bell = jnp.exp(-0.5 * (hidden * hidden)) * (1.0 / math.sqrt(2 * math.pi))
    return hidden * cdf, cdf + hidden * bell


def mlp_kernel(
    chunk, side_ref, mlp_ref, bg_ref, mlp_t_ref, bg_t_ref, up_ref, bup_ref, down_ref,
    keep_ref, send_ref, out_ref, din_ref, bupg_ref, act_s, hg_s,
):
    tokens, width = mlp_ref.shape

    @pl.when(pl.program_id(0) == 0)
    def _():
        out_ref[...] = jnp.zeros_like(out_ref)
        din_ref[...] = jnp.zeros_like(din_ref)

    bupg_ref[...] = jnp.zeros_like(bupg_ref)
    bias = bup_ref[...].astype(F32)

    def step(i, carry):
        at = pl.ds(pl.multiple_of(i * chunk, chunk), chunk)
        hidden = matmul(mlp_ref[at, :], up_ref[...]) + bias
        back = matmul(bg_ref[at, :], down_ref[...], NT)
        act, slope = gelu_parts(hidden)
        act = act.astype(BF)
        hg = (back * slope).astype(BF)
        act_s[at, :] = act
        hg_s[at, :] = hg
        bupg_ref[...] += jnp.sum(hg.astype(F32), axis=0, keepdims=True)
        out_ref[at, :] += matmul(act, down_ref[...])
        din_ref[at, :] += matmul(hg, up_ref[...], NT)
        return carry

    lax.fori_loop(0, tokens // chunk, step, 0)
    half = width // 2
    side = side_ref[0]
    mine = pl.ds(pl.multiple_of(side * half, half), half)
    other = pl.ds(pl.multiple_of((1 - side) * half, half), half)
    send_ref[0] = matmul(mlp_t_ref[other, :], hg_s[...]).astype(BF)
    send_ref[1] = matmul(bg_t_ref[other, :], act_s[...]).astype(BF)
    keep_ref[0] = matmul(mlp_t_ref[mine, :], hg_s[...]).astype(BF)
    keep_ref[1] = matmul(bg_t_ref[mine, :], act_s[...]).astype(BF)


def attention_kernel(
    heads, head_size, seq_devices, first_row, where_ref, seg_ref, q_t_ref, g_t_ref, even_ref,
    odd_ref, cos_ref, sin_ref, *refs,
):
    (mix_t_ref, qpg_t_ref, dkeep_ref, dsend_ref, kv_s, kv_t_s, bias_s, p_s, ds_s, gk_s, o_s, dq_s,
     dkv_s, m_s, l_s, d_s, mk_s) = refs[-17:]
    length = seg_ref.shape[-1]
    me = where_ref[0]
    start = me * length
    group = math.gcd(heads, 3)

    def columns(h, count=1):
        return slice(h * length, (h + count) * length)

    def head(h):
        return slice(h * head_size, (h + 1) * head_size)

    counts = jnp.zeros((1, LANES), F32)
    for m in range(seq_devices):
        ref = (even_ref, odd_ref)[m % 2]
        at = pl.multiple_of((me ^ m) * length, length)
        kv_s[pl.ds(at, length), :] = ref[m // 2, 0, :length]
        counts = counts + ref[m // 2, 0, length : length + COUNT_ROWS].astype(F32)[:1]

    segments = seg_ref[pl.ds(first_row + pl.program_id(0), 1), :]
    low = jnp.zeros((1, length), F32)
    for c in range(DOCS):
        later = (segments > c) | (segments < 0)
        low = low + jnp.where(later, counts[:, c : c + 1], 0.0)
    low = low.astype(jnp.int32)
    first_block = jnp.min(low) // KEY_BLOCK
    end_block = (start + length - 1) // KEY_BLOCK + 1
    place = start + lax.broadcasted_iota(jnp.int32, (1, length), 1)

    m_s[...] = jnp.full_like(m_s, NEGATIVE)
    l_s[...] = jnp.zeros_like(l_s)
    o_s[...] = jnp.zeros_like(o_s)
    dq_s[...] = jnp.zeros_like(dq_s)
    dkv_s[...] = jnp.zeros_like(dkv_s)

    def forward(b, carry):
        at = pl.multiple_of(b * KEY_BLOCK, KEY_BLOCK)
        kv = kv_s[pl.ds(at, KEY_BLOCK), :]
        keys = kv[:, :head_size]
        kv_t = kv.astype(F32).T.astype(BF)
        kv_t_s[b] = kv_t
        summed = jnp.concatenate([kv_t[head_size:], jnp.ones((16, KEY_BLOCK), BF)], axis=0)
        key_place = at + lax.broadcasted_iota(jnp.int32, (KEY_BLOCK, length), 0)
        allowed = (key_place <= place) & (key_place >= low)
        bias_s[...] = jnp.where(allowed, 0.0, NEGATIVE)
        bias = bias_s[...]
        shrinks = {}

        def scores(h):
            return matmul(keys, q_t_ref[0, :, columns(h, group)])

        def mix(h):
            o = matmul(summed, p_s[b, :, columns(h, group)])
            for j in range(group):
                row = slice(h + j, h + j + 1)
                part = o[:, columns(j)]
                shrink = shrinks.pop(h + j)
                o_s[:, columns(h + j)] = o_s[:, columns(h + j)] * shrink + part[:head_size]
                l_s[row, :] = l_s[row, :] * shrink + part[head_size : head_size + 1]

        ready = scores(0)
        for h in range(0, heads, group):
            now_scores = ready
            if h + group < heads:
                ready = scores(h + group)
            for j in range(group):
                row = slice(h + j, h + j + 1)
                s = now_scores[:, columns(j)] + bias
                before = m_s[row, :]
                now = jnp.maximum(before, jnp.max(s, axis=0, keepdims=True))
                p_s[b, :, columns(h + j)] = jnp.exp(s - now).astype(BF)
                shrinks[h + j] = jnp.exp(before - now)
                m_s[row, :] = now
                mk_s[b, row, :] = now
            if h > 0:
                mix(h - group)
        mix(heads - group)
        return carry

    lax.fori_loop(first_block, end_block, forward, 0)

    for h in range(heads):
        row = slice(h, h + 1)
        inverse = 1.0 / l_s[row, :]
        mixed = o_s[:, columns(h)] * inverse
        mix_t_ref[head(h), :] = mixed.astype(BF)
        d_s[row, :] = jnp.sum(
            mixed * g_t_ref[0, :, columns(h)].astype(F32), axis=0, keepdims=True
        )
        l_s[row, :] = inverse

    def backward(b, carry):
        at = pl.multiple_of(b * KEY_BLOCK, KEY_BLOCK)
        values = kv_s[pl.ds(at, KEY_BLOCK), :][:, head_size:]
        keys_t = kv_t_s[b][:head_size]
        inners = {}

        def prob_grads(h):
            for j in range(group):
                row = slice(h + j, h + j + 1)
                factor = jnp.exp(mk_s[b, row, :] - m_s[row, :]) * l_s[row, :]
                scaled = g_t_ref[0, :, columns(h + j)].astype(F32) * factor
                gk_s[:, columns(h + j)] = scaled.astype(BF)
                inners[h + j] = d_s[row, :] * factor
            return matmul(values, gk_s[:, columns(h, group)])

        ready = prob_grads(0)
        for h in range(0, heads, group):
            now_grads = ready
            if h + group < heads:
                ready = prob_grads(h + group)
            for j in range(group):
                p = p_s[b, :, columns(h + j)].astype(F32)
                ds_s[:, columns(h + j)] = (
                    p * (now_grads[:, columns(j)] - inners.pop(h + j))
                ).astype(BF)
        dq_s[...] += matmul(keys_t, ds_s[...])
        dk = matmul(ds_s[...], q_t_ref[0], NT)
        dv = matmul(p_s[b], gk_s[...], NT)
        dkv_s[pl.ds(at, KEY_BLOCK), :] = jnp.concatenate([dk, dv], axis=1).astype(BF)
        return carry

    lax.fori_loop(first_block, end_block, backward, 0)

    cosine, sine = cos_ref[...], sin_ref[...]
    score_scale = 1.0 / math.sqrt(head_size)
    for h in range(heads):
        qpg_t_ref[head(h), :] = turn(
            dq_s[:, columns(h)] * score_scale, cosine, -sine
        ).astype(BF)
    for m in range(seq_devices):
        ref = (dkeep_ref, dsend_ref)[m % 2]
        at = pl.multiple_of((me ^ m) * length, length)
        ref[m // 2, 0] = dkv_s[pl.ds(at, length), :]


def mix_kernel(
    side_ref, tok_ref, seg_ref, mix_t_ref, qpg_t_ref, attn_t_ref, bg_t_ref, mlp_ref, wo_ref,
    bo_ref, bd_ref, out_ref, keep_ref, send_ref, acc_q, acc_o,
):
    step, steps = pl.program_id(0), pl.num_programs(0)

    @pl.when(step == 0)
    def _():
        acc_q[...] = jnp.zeros_like(acc_q)
        acc_o[...] = jnp.zeros_like(acc_o)

    mix_t = mix_t_ref[...]
    branch = matmul(mix_t, wo_ref[...], TN) + (row_of(bo_ref) + row_of(bd_ref)) + mlp_ref[...]
    valid = valid_column(seg_ref[pl.ds(step, 1), :])
    out_ref[0] = (tok_ref[0].astype(F32) + valid * branch).astype(BF)
    acc_q[...] += matmul(attn_t_ref[...], qpg_t_ref[...], NT)
    acc_o[...] += matmul(bg_t_ref[...], mix_t, NT)

    @pl.when(step == steps - 1)
    def _():
        half = acc_q.shape[0] // 2
        side = side_ref[0]
        mine = pl.ds(pl.multiple_of(side * half, half), half)
        other = pl.ds(pl.multiple_of((1 - side) * half, half), half)
        for j, acc in enumerate((acc_q, acc_o)):
            keep_ref[j] = acc[mine, :].astype(BF)
            send_ref[j] = acc[other, :].astype(BF)


def exit_kernel(
    order_a, rows, permuted,
    side_ref, tok_ref, og_ref, seg_ref, qpg_t_ref, attn_t_ref, din_ref, wq_ref, wkv_ref,
    ag_ref, mg_ref, cos_ref, sin_ref, bupg_ref, shuffle_ref, dkv_refs,
    tg_ref, keep_ref, send_ref, acc, vec,
):
    step, steps = pl.program_id(0), pl.num_programs(0)

    @pl.when(step == 0)
    def _():
        acc[...] = jnp.zeros_like(acc)
        vec[...] = jnp.zeros_like(vec)

    dkv = sum((ref[0].astype(F32) for ref in dkv_refs[1:]), dkv_refs[0][0].astype(F32))
    kvpg_t = turn(dkv.T, cos_ref[...], -sin_ref[...]).astype(BF)
    acc[...] += matmul(attn_t_ref[...], kvpg_t, NT)
    qpg_t = qpg_t_ref[...]
    d_attn = (matmul(wq_ref[...], qpg_t) + matmul(wkv_ref[...], kvpg_t)).T
    d_mlp = din_ref[...]
    n, scale = norm_parts(tok_ref[0].astype(F32))
    og = og_ref[0].astype(F32)
    e = d_attn * row_of(ag_ref) + d_mlp * row_of(mg_ref)
    inner = jnp.mean(e * n, axis=-1, keepdims=True)
    tg_ref[0] = (og + scale * (e - jnp.mean(e, axis=-1, keepdims=True) - n * inner)).astype(BF)
    ones = jnp.ones((8, qpg_t.shape[1]), BF)
    bg = (og * valid_column(seg_ref[pl.ds(step, 1), :])).astype(BF)
    sums = [d_attn * n, d_attn, d_mlp * n, d_mlp, None, bg.astype(F32)]
    for j, value in enumerate(sums):
        if value is None:
            part = matmul(ones, qpg_t, NT)[:1]
        else:
            part = jnp.sum(value, axis=0, keepdims=True)
        vec[j : j + 1, :] += part

    @pl.when(step == steps - 1)
    def _():
        vec[8:12, :] = bupg_ref[...]
        if permuted:
            columns = permute_rows(vec[...].T, order_a, rows)
        else:
            columns = lax.dot_general(
                shuffle_ref[...], vec[...], NT, precision=lax.Precision.HIGHEST,
                preferred_element_type=F32,
            )
        half = columns.shape[0] // 2
        acc_columns = slice(0, LANES)
        vec_columns = slice(LANES, 2 * LANES)
        for side in range(2):

            @pl.when(side_ref[0] == side)
            def _():
                mine = slice(side * half, (side + 1) * half)
                other = slice((1 - side) * half, (2 - side) * half)
                keep_ref[:, acc_columns] = acc[mine, :].astype(BF)
                send_ref[:, acc_columns] = acc[other, :].astype(BF)
                keep_ref[:, vec_columns] = columns[mine].astype(BF)
                send_ref[:, vec_columns] = columns[other].astype(BF)


def partners(size, mask):
    return [(i, i ^ mask) for i in range(size)]


class Stream:
    def __init__(self, arrays, count, resident, width):
        self.terms = [(array, resident, 0, at, ()) for array, at in arrays]
        self.count, self.resident, self.width = count, resident, width
        self.rows = arrays[0][0].shape[1]

    def halve(self, bit):
        count = self.count = self.count // 2
        mine, other = [], []
        for array, resident, column, at, adds in self.terms:
            mine.append((array, resident, column, at, adds + ((bit, count),)))
            other.append((array, resident, column, at + count, adds + ((bit, -count),)))
        self.terms = mine
        return other


def first_block(term, where_ref):
    at = term[3]
    for (axis, bit), weight in term[4]:
        at = at + ((where_ref[axis] >> bit) & 1) * weight
    return at


def term_spec(term, width, group):
    if term[1]:
        return pl.BlockSpec(memory_space=pltpu.VMEM)
    return pl.BlockSpec(
        (group, term[0].shape[1], width),
        lambda i, where_ref: (first_block(term, where_ref) // group + i, 0, term[2] // width),
    )


def in_hbm(value):
    return pltpu.with_memory_space_constraint(value, pltpu.HBM)


def operands_of(terms):
    return [term[0] if term[1] else in_hbm(term[0]) for term in terms]


def read_terms(terms, refs, width, group, where_ref):
    total = None
    for term, ref in zip(terms, refs):
        if term[1]:
            at = first_block(term, where_ref) + pl.program_id(0) * group
            value = ref[pl.ds(at, group), :, term[2] : term[2] + width]
        else:
            value = ref[...]
        value = value.astype(F32)
        total = value if total is None else total + value
    return total


def call_on_terms(
    body, name, where, after, steps, in_specs, operands, out_specs, out_shape, length
):
    return pl.pallas_call(
        body,
        grid_spec=pltpu.PrefetchScalarGridSpec(
            num_scalar_prefetch=1, grid=(steps,), in_specs=in_specs, out_specs=out_specs
        ),
        out_shape=out_shape,
        compiler_params=params(limit=24),
        cost_estimate=length,
        name=name,
    )(ordered_after(where, *after), *operands)


def sums_to_send(picks, streams, joined, where, after, length):
    count, rows, resident = streams[0].count, streams[0].rows, streams[0].resident
    widths = [streams[j % len(streams)].width for j in range(len(picks))]
    group = count
    while group > 1 and group * widths[0] > 4 * 3072 and not resident:
        group //= 2
    terms = [term for pick in picks for term in pick]
    outputs = len(picks) // joined
    shapes = [(rows, sum(widths[j * joined : (j + 1) * joined])) for j in range(outputs)]

    def body(where_ref, *refs):
        at = 0
        for j, (pick, width) in enumerate(zip(picks, widths)):
            total = read_terms(pick, refs[at : at + len(pick)], width, group, where_ref).astype(BF)
            column = sum(widths[j - j % joined : j])
            refs[len(terms) + j // joined][:, :, column : column + width] = total
            at += len(pick)

    if resident:
        out_specs = [pl.BlockSpec(memory_space=pltpu.VMEM) for _ in shapes]
    else:
        out_specs = [pl.BlockSpec((group,) + shape, lambda i, _: (i, 0, 0)) for shape in shapes]
    return call_on_terms(
        body, "combine", where, after, count // group,
        [term_spec(term, width, group) for pick, width in zip(picks, widths) for term in pick],
        operands_of(terms),
        out_specs,
        [jax.ShapeDtypeStruct((count,) + shape, BF) for shape in shapes],
        length or short(2 * count * rows * sum(len(p) * w for p, w in zip(picks, widths))),
    )


def own_sums(streams, where, after=(), length=None, vectors=()):
    terms = [term for stream in streams for term in stream.terms]
    shapes = [(stream.rows, stream.width) for stream in streams]
    if vectors:
        shapes[-1] = (shapes[-1][0], shapes[-1][1] - LANES)
        shapes += [(streams[-1].rows,)] * len(vectors)

    def body(where_ref, *refs):
        at = 0
        for stream, output in zip(streams, refs[len(terms) :]):
            size = len(stream.terms)
            total = read_terms(stream.terms, refs[at : at + size], stream.width, 1, where_ref)[0]
            output[...] = total[:, : output.shape[1]]
            at += size
        if vectors:
            turned = total[:, -LANES:].T
            for row, output in zip(vectors, refs[len(terms) + len(streams) :]):
                output[...] = turned[row : row + 1].reshape(output.shape)

    return call_on_terms(
        body, "own", where, after, 1,
        [term_spec(term, stream.width, 1) for stream in streams for term in stream.terms],
        operands_of(terms),
        [whole(shape) for shape in shapes],
        [jax.ShapeDtypeStruct(shape, F32) for shape in shapes],
        length or short(2 * len(terms) * streams[0].rows * streams[0].width),
    )


def ordered_after(value, *others):
    if not others:
        return value
    return lax.optimization_barrier((value, others))[0]


AXES = ("seq", "batch")


def reduce_level(streams, bits, where, after=(), length=None):
    picks = [stream.halve(bit) for stream, bit in zip(streams, bits)]
    joined = len(set(bits)) == 1
    sends = sums_to_send(picks, streams, len(streams) if joined else 1, where, after, length)
    recvs = []
    for (axis, bit), send in zip(bits, sends):
        recvs.append(
            lax.ppermute(send, AXES[axis], partners(lax.axis_size(AXES[axis]), 1 << bit))
        )
    for j, stream in enumerate(streams):
        column = j * stream.width if joined else 0
        resident = stream.resident or stream.count <= 4
        stream.terms.append((recvs[0 if joined else j], resident, column, 0, ()))
    return sends, recvs


def exchange(streams, bits, where, after=()):
    axis = AXES[bits[0][0]]
    picks, recvs = [], []
    for mask in range(1, 1 << len(bits)):
        for stream in streams:
            count, terms = stream.count, stream.terms
            for j, bit in enumerate(bits):
                count //= 2
                sign, shift = (-1, count) if (mask >> j) & 1 else (1, 0)
                terms = [
                    (a, r, c, at + shift, adds + ((bit, sign * count),))
                    for a, r, c, at, adds in terms
                ]
            picks.append(terms)
    for stream in streams:
        for bit in bits:
            stream.halve(bit)
    sends = sums_to_send(picks, streams, len(streams), where, after, None)
    for mask, send in enumerate(sends, 1):
        partner = sum(((mask >> j) & 1) << bit[1] for j, bit in enumerate(bits))
        recv = lax.ppermute(send, axis, partners(lax.axis_size(axis), partner))
        column = 0
        for stream in streams:
            stream.terms.append((recv, stream.resident, column, 0, ()))
            column += stream.width
    return sends


def on_device(
    tokens, segment_ids, attn_gain, attn_shift, mlp_gain, mlp_shift, w_query, b_query,
    w_keyvalue, w_out, b_out, w_up, b_up, w_down, b_down, out_grad,
):
    row_count, length, width = tokens.shape
    head_size = w_keyvalue.shape[1] // 2
    heads = width // head_size
    hidden = w_up.shape[1]
    token_count = row_count * length
    seq_devices = lax.axis_size("seq")
    batch_devices = lax.axis_size("batch")
    devices = seq_devices * batch_devices
    seq_index = lax.axis_index("seq").astype(jnp.int32)
    batch_index = lax.axis_index("batch").astype(jnp.int32)
    side = (seq_index & 1).reshape(1)
    where = jnp.stack([seq_index, batch_index])
    rows = width // devices
    permuted = rows % 8 == 0
    seq_bits = list(range(seq_devices.bit_length() - 1))

    def reversed_bits(value, count):
        return sum(((value >> j) & 1) << (count - 1 - j) for j in range(count))

    batch_order = [
        reversed_bits(z, batch_devices.bit_length() - 1) for z in range(batch_devices)
    ]

    def device_order(bits):
        order = []
        for k in range(seq_devices):
            at = 0
            for j, bit in enumerate(bits):
                at |= ((k >> (len(bits) - 1 - j)) & 1) << bit
            order += [z * seq_devices + at for z in batch_order]
        return order

    order_a = device_order(seq_bits)
    order_b = device_order(seq_bits[:1] + seq_bits[:0:-1])

    def ordered(values, order):
        if permuted:
            return values
        shaped = values.reshape(values.shape[:-2] + (devices, rows, values.shape[-1]))
        return jnp.take(shaped, jnp.array(order), axis=-3).reshape(values.shape)

    positions = (seq_index * length + jnp.arange(length)).astype(F32)
    inverse = 10000.0 ** (-(jnp.arange(HALF_ROT).astype(F32) * (2.0 / ROT_DIMS)))
    angles = inverse[:, None] * positions[None, :]
    cosine, sine = jnp.cos(angles), jnp.sin(angles)
    segments_spec = whole((row_count, length))
    turn_spec = whole((HALF_ROT, length))
    width_spec = whole((width,))

    def row_block(shape, first=0):
        return pl.BlockSpec((1,) + shape, lambda r, *_: (first + r, 0, 0))

    token_block = pl.BlockSpec((length, width), lambda r, *_: (r, 0))
    whole_lanes = length % LANES == 0

    def column_block(first=0):
        if whole_lanes:
            return pl.BlockSpec((width, length), lambda r, *_: (0, first + r))
        return pl.BlockSpec((None, width, length), lambda r, *_: (first + r, 0, 0))

    columns = jax.ShapeDtypeStruct(
        (width, token_count) if whole_lanes else (row_count, width, length), BF
    )

    def joined(values):
        if whole_lanes:
            return values
        return jnp.transpose(values, (1, 0, 2)).reshape(width, token_count)

    lanes = heads * length
    mlp_in, bg, mlp_t, bg_t, attn_t, q_t, g_t, keyvalue, payload = pl.pallas_call(
        functools.partial(entry_kernel, head_size, order_a, order_b, rows, permuted),
        grid=(row_count,),
        in_specs=[
            row_block((length, width)), row_block((length, width)), segments_spec,
            width_spec, width_spec, width_spec, width_spec, width_spec,
            whole((width, width)), whole((width, 2 * head_size)), whole((width, width)),
            turn_spec, turn_spec,
        ],
        out_specs=[
            token_block, token_block, column_block(), column_block(), column_block(),
            row_block((head_size, lanes)), row_block((head_size, lanes)),
            row_block((length, 2 * head_size)), row_block((length + COUNT_ROWS, 2 * head_size)),
        ],
        out_shape=[
            jax.ShapeDtypeStruct((token_count, width), BF),
            jax.ShapeDtypeStruct((token_count, width), BF),
            columns,
            columns,
            columns,
            jax.ShapeDtypeStruct((row_count, head_size, lanes), BF),
            jax.ShapeDtypeStruct((row_count, head_size, lanes), BF),
            jax.ShapeDtypeStruct((row_count, length, 2 * head_size), BF),
            jax.ShapeDtypeStruct((row_count, length + COUNT_ROWS, 2 * head_size), BF),
        ],
        compiler_params=params(60),
        cost_estimate=LONG,
        name="entry",
    )(
        tokens, out_grad, segment_ids, attn_gain, attn_shift, mlp_gain, mlp_shift, b_query,
        w_query, w_keyvalue, w_out, cosine, sine,
    )
    mlp_t, attn_t = ordered(mlp_t, order_a), ordered(attn_t, order_a)
    bg_t = ordered(bg_t, order_b)

    gathered = [payload]
    for mask in range(2, seq_devices, 2):
        gathered.append(lax.ppermute(payload, "seq", partners(seq_devices, mask)))

    tile = math.gcd(512, hidden)
    half = width // 2
    pair_cols = pl.BlockSpec((2, half, tile), lambda f, *_: (0, 0, f))
    pair_shape = jax.ShapeDtypeStruct((2, half, hidden), BF)
    keep, send, mlp_out, mlp_din, b_up_part = pl.pallas_call(
        functools.partial(mlp_kernel, token_count),
        grid_spec=pltpu.PrefetchScalarGridSpec(
            num_scalar_prefetch=1,
            grid=(hidden // tile,),
            in_specs=[
                whole((token_count, width)), whole((token_count, width)),
                whole((width, token_count)), whole((width, token_count)),
                pl.BlockSpec((width, tile), lambda f, *_: (0, f)),
                pl.BlockSpec((1, tile), lambda f, *_: (0, f)),
                pl.BlockSpec((tile, width), lambda f, *_: (f, 0)),
            ],
            out_specs=[
                pair_cols, pair_cols, whole((token_count, width)), whole((token_count, width)),
                pl.BlockSpec((1, tile), lambda f, *_: (0, f)),
            ],
            scratch_shapes=[
                pltpu.VMEM((token_count, tile), BF), pltpu.VMEM((token_count, tile), BF),
            ],
        ),
        out_shape=[
            pair_shape, pair_shape,
            jax.ShapeDtypeStruct((token_count, width), F32),
            jax.ShapeDtypeStruct((token_count, width), F32),
            jax.ShapeDtypeStruct((1, hidden), F32),
        ],
        compiler_params=params(60),
        cost_estimate=LONG,
        name="mlp",
    )(side, mlp_in, bg, joined(mlp_t), joined(bg_t), w_up, b_up.reshape(1, hidden), w_down)

    gathered = ordered_after(tuple(gathered), b_up_part)

    def stack_body(*refs):
        for j, ref in enumerate(refs[:-1]):
            refs[-1][j] = ref[...]

    even = pl.pallas_call(
        stack_body,
        in_specs=[pl.BlockSpec(memory_space=pltpu.VMEM)] * len(gathered),
        out_specs=pl.BlockSpec(memory_space=pltpu.VMEM),
        out_shape=jax.ShapeDtypeStruct((len(gathered),) + payload.shape, BF),
        compiler_params=pltpu.CompilerParams(vmem_limit_bytes=24 * 1024 * 1024),
        cost_estimate=LONGEST,
        name="stack",
    )(*gathered)
    odd = lax.ppermute(even, "seq", partners(seq_devices, 1))

    bits = [(0, bit) for bit in range(1, seq_devices.bit_length() - 1)]
    batch_bits = [(1, bit) for bit in range(batch_devices.bit_length() - 1)]
    blocks = devices // 2

    def pair_streams(keep, send, resident):
        shape = (2 * blocks, rows, keep.shape[2])
        keep = keep.reshape(shape)
        recv = lax.ppermute(send.reshape(shape), "seq", partners(seq_devices, 1))
        return [
            Stream([(keep, at), (recv, at)], blocks, resident, keep.shape[2])
            for at in (0, blocks)
        ]

    mlp_streams = pair_streams(keep, send, False)

    half_seq = seq_devices // 2
    key_blocks = length * seq_devices // KEY_BLOCK
    stat_rows = -(-heads // 8) * 8

    def attention(first, count, after, before):
        kv_rows = pl.BlockSpec(
            (half_seq, 1, length + COUNT_ROWS, 2 * head_size), lambda r, *_: (0, first + r, 0, 0)
        )
        dkv_rows = pl.BlockSpec(
            (half_seq, 1, length, 2 * head_size), lambda r, *_: (0, first + r, 0, 0)
        )
        dkv_shape = jax.ShapeDtypeStruct((half_seq, row_count, length, 2 * head_size), BF)
        return pl.pallas_call(
            functools.partial(attention_kernel, heads, head_size, seq_devices, first),
            grid_spec=pltpu.PrefetchScalarGridSpec(
                num_scalar_prefetch=1,
                grid=(count,),
                in_specs=[
                    segments_spec, row_block((head_size, lanes), first),
                    row_block((head_size, lanes), first), kv_rows, kv_rows, turn_spec, turn_spec,
                ]
                + [pl.BlockSpec(memory_space=pl.ANY)] * len(before),
                out_specs=[column_block(first), column_block(first), dkv_rows, dkv_rows],
                scratch_shapes=[
                    pltpu.VMEM((key_blocks * KEY_BLOCK, 2 * head_size), BF),
                    pltpu.VMEM((key_blocks, 2 * head_size, KEY_BLOCK), BF),
                    pltpu.VMEM((KEY_BLOCK, length), F32),
                    pltpu.VMEM((key_blocks, KEY_BLOCK, lanes), BF),
                    pltpu.VMEM((KEY_BLOCK, lanes), BF),
                    pltpu.VMEM((head_size, lanes), BF),
                    pltpu.VMEM((head_size, lanes), F32),
                    pltpu.VMEM((head_size, lanes), F32),
                    pltpu.VMEM((key_blocks * KEY_BLOCK, 2 * head_size), BF),
                    pltpu.VMEM((stat_rows, length), F32),
                    pltpu.VMEM((stat_rows, length), F32),
                    pltpu.VMEM((stat_rows, length), F32),
                    pltpu.VMEM((key_blocks, stat_rows, length), F32),
                ],
            ),
            out_shape=[columns, columns, dkv_shape, dkv_shape],
            input_output_aliases={8 + j: j for j in range(len(before))},
            compiler_params=params(60),
            cost_estimate=LONG,
        name="attention",
        )(
            ordered_after(where, *after), segment_ids, q_t, g_t, in_hbm(even), in_hbm(odd), cosine,
            sine, *before,
        )

    pair_levels = [(bits[i], bits[-1 - i]) for i in range(len(bits))]
    batch_levels = [(bit, bit) for bit in batch_bits]
    mlp_levels = iter(pair_levels + batch_levels)
    results, first_row = [b_up_part], 0
    last_share = max(row_count // 4, 1)
    for share in (row_count - last_share, last_share):
        after = results[:1] if first_row else [even]
        after, _ = reduce_level(mlp_streams, next(mlp_levels), where, after, LONG)
        results = attention(first_row, share, after, results if first_row else [])
        first_row += share
    mix_t, qpg_t, dkv_keep, dkv_send = results
    dkv_recv = lax.ppermute(dkv_send, "seq", partners(seq_devices, 1))
    after, mlp_recv = reduce_level(mlp_streams, next(mlp_levels), where, [mix_t], LONG)

    def share_body(where_ref, keep_ref, recv_ref, *out_refs):
        for j, out_ref in enumerate(out_refs):
            out_ref[...] = (keep_ref[j].astype(F32) + recv_ref[j].astype(F32)).astype(BF)

    shares = call_on_terms(
        share_body, "share", where, after, 1,
        [pl.BlockSpec(memory_space=pltpu.VMEM)] * 2, [dkv_keep, dkv_recv],
        [pl.BlockSpec(memory_space=pltpu.VMEM)] * half_seq,
        [jax.ShapeDtypeStruct(dkv_keep.shape[1:], BF)] * half_seq,
        short(6 * dkv_keep.size),
    )
    dkv_parts = [shares[0]]
    for j in range(1, half_seq):
        dkv_parts.append(lax.ppermute(shares[j], "seq", partners(seq_devices, 2 * j)))

    pair_spec = pl.BlockSpec(memory_space=pltpu.VMEM)
    pair_width = jax.ShapeDtypeStruct((2, half, width), BF)
    output, keep, send = pl.pallas_call(
        mix_kernel,
        grid_spec=pltpu.PrefetchScalarGridSpec(
            num_scalar_prefetch=1,
            grid=(row_count,),
            in_specs=[
                row_block((length, width)), segments_spec, column_block(), column_block(),
                column_block(), column_block(), token_block, whole((width, width)),
                width_spec, width_spec,
            ],
            out_specs=[row_block((length, width)), pair_spec, pair_spec],
            scratch_shapes=[pltpu.VMEM((width, width), F32), pltpu.VMEM((width, width), F32)],
        ),
        out_shape=[
            jax.ShapeDtypeStruct((row_count, length, width), BF), pair_width, pair_width,
        ],
        compiler_params=params(56),
        cost_estimate=LONG,
        name="mix",
    )(
        ordered_after(side, dkv_parts[0]), tokens, segment_ids, mix_t, qpg_t, attn_t, bg_t,
        mlp_out, w_out, b_out, b_down,
    )
    mix_streams = pair_streams(keep, send, True)
    after = [keep, *mlp_recv, *dkv_parts[1:]]
    after, _ = reduce_level(mlp_streams, next(mlp_levels), where, after, LONG)
    after, _ = reduce_level(mix_streams, pair_levels[0], where, after)

    dkv_count = len(dkv_parts)

    def exit_body(*refs):
        fixed, rest = refs[:15], refs[15:]
        exit_kernel(order_a, rows, permuted, *fixed, rest[:dkv_count], *rest[dkv_count:])

    if permuted:
        shuffle = jnp.zeros((8, LANES), F32)
    else:
        places = (jnp.array(order_a)[:, None] * rows + jnp.arange(rows)[None, :]).reshape(width, 1)
        shuffle = (places == jnp.arange(width)[None, :]).astype(F32)
    b_up_rows = jnp.transpose(
        b_up_part.reshape(devices, hidden // width, rows), (1, 0, 2)
    ).reshape(hidden // width, width)
    extra_spec = pl.BlockSpec(memory_space=pltpu.VMEM)
    extra_shape = jax.ShapeDtypeStruct((half, 2 * LANES), BF)
    tokens_grad, keep, send = pl.pallas_call(
        exit_body,
        grid_spec=pltpu.PrefetchScalarGridSpec(
            num_scalar_prefetch=1,
            grid=(row_count,),
            in_specs=[
                row_block((length, width)), row_block((length, width)), segments_spec,
                column_block(), column_block(), token_block, whole((width, width)),
                whole((width, 2 * head_size)), width_spec, width_spec, turn_spec, turn_spec,
                whole((hidden // width, width)), whole(shuffle.shape),
            ]
            + [row_block((length, 2 * head_size))] * dkv_count,
            out_specs=[row_block((length, width)), extra_spec, extra_spec],
            scratch_shapes=[
                pltpu.VMEM((width, 2 * head_size), F32), pltpu.VMEM((LANES, width), F32),
            ],
        ),
        out_shape=[
            jax.ShapeDtypeStruct((row_count, length, width), BF), extra_shape, extra_shape,
        ],
        compiler_params=params(56),
        cost_estimate=LONG,
        name="exit",
    )(
        ordered_after(side, *after), tokens, out_grad, segment_ids, qpg_t, attn_t, mlp_din, w_query, w_keyvalue,
        attn_gain, mlp_gain, cosine, sine, b_up_rows, shuffle,
        *dkv_parts,
    )

    shape = (blocks, rows, 2 * LANES)
    keep = keep.reshape(shape)
    recv = lax.ppermute(send.reshape(shape), "seq", partners(seq_devices, 1))
    extra_streams = [Stream([(keep, 0), (recv, 0)], blocks, True, 2 * LANES)]
    after = [keep]
    for level in pair_levels[1:]:
        after, _ = reduce_level(mix_streams, level, where, after)
    after = exchange(extra_streams, bits, where, after)[:1]
    for level in mlp_levels:
        after, _ = reduce_level(mlp_streams, level, where, after)
    sums = own_sums(mlp_streams, where, after, LONG)
    small_streams = mix_streams + extra_streams
    exchange(small_streams, batch_bits, where, sums[:1])
    several = hidden // width
    sums += own_sums(small_streams, where, vectors=[*range(6), *range(8, 8 + several)])
    w_up_grad, w_down_grad_t, w_query_grad, w_out_grad_t, w_keyvalue_grad, *vectors = sums
    return (
        output,
        keyvalue,
        tokens_grad,
        vectors[0],
        vectors[1],
        vectors[2],
        vectors[3],
        w_query_grad,
        vectors[4],
        w_keyvalue_grad,
        w_out_grad_t.T,
        vectors[5],
        w_up_grad,
        jnp.concatenate(vectors[6:]),
        w_down_grad_t.T,
        vectors[5],
    )


def solution(mesh):
    row_spec = P("batch", "seq", None)
    split = P(("batch", "seq"))
    first = P(("batch", "seq"), None)
    last = P(None, ("batch", "seq"))
    return jax.shard_map(
        on_device,
        mesh=mesh,
        in_specs=(row_spec, P("batch", "seq")) + (P(),) * 13 + (row_spec,),
        out_specs=(
            row_spec, row_spec, row_spec, split, split, split, split, first, split, first, last,
            split, first, split, last, split,
        ),
        check_vma=False,
    )
```

profile of v0, /device:TPU:0, one launch (start us, length us, event | category | flops | bytes accessed | tf_op | source)
XLA Modules:
  0.0 190.9 jit_solution(5227833891552975405)
XLA Ops:
  1.4 9.0 %entry.1 = (bf16[1024,768]{1,0:T(8,128)(2,1)}, bf16[1024,768]{1,0:T(8,128)(2,1)}, bf16[768,1024]{1,0:T(8,128)(2,1)}, bf16[768,1024]{1,0:T(8,128)(2,1)}, bf16[768...) custom-call(bf16[4,256,768]{2,1,0:T(8,128)(2,1)} %refs_1_.1, ...), custom_call_target="tpu_custom_call" | custom-call | flops 40000000000 | bytes 10000000 | tf_op jit(solution)/shard_map/entry/pallas_call | solution.py:662
  10.4 3.0 %collective-permute-start = (bf16[4,272,128]{2,1,0:T(8,128)(2,1)}, bf16[4,272,128]{2,1,0:T(8,128)(2,1)S(1)}, u32[]{:S(2)}, u32[]{:S(2)}) collective-permute-start(bf16[4,272,128]{2,1,0:T(8,128)(2,1)} %get-tuple-element.101.refs_0_), channel_id=1, source_target_pairs={{0,2},{1,3},{2,0},{3,1},{4,6},{5,7},{6,4},{7,5},{8,10},{9,11},{10,... | collective-permute-start | bytes 835592 | tf_op jit(solution)/shard_map/ppermute | solution.py:699
  13.4 1.5 collective-permute-start.1
  15.6 37.8 %mlp.1 = (bf16[2,384,3072]{2,1,0:T(8,128)(2,1)}, bf16[2,384,3072]{2,1,0:T(8,128)(2,1)}, f32[1024,768]{1,0:T(8,128)}, f32[1024,768]{1,0:T(8,128)}, f32[1,3072]{1,0:T(1,128)}) custom-call(s32[1]{0:T(128)} %bitcast.side_ref.refs_0_, bf16[1024,768]{1,0:T(8,128)(2,1)} %get-tuple-element.96.mlp_ref, bf16[1024,768]{1,0:T(8,128)(2,1)} %get-tuple-element.97.bg_ref, ...), custom_call_target="tpu_custom_call" | custom-call | flops 40000000000 | bytes 10000000 | tf_op jit(solution)/shard_map/mlp/pallas_call | solution.py:705
  54.0 1.4 reduce.3
  57.0 4.7 %collective-permute-done.3.refs_1_.refs_3_.refs_4_.refs_5_.refs_6_.refs_7_ = bf16[32,24,3072]{2,1,0:T(8,128)(2,1)} collective-permute-done((bf16[32,24,3072]{2,1,0:T(8,128)(2,1)}, bf16[32,24,3072]{2,1,0:T(8,128)(2,1)}, u32[]{:S(2)}, u32[]{:S(2)}) %collective-permute-start.3) | collective-permute-done | bytes 4718624 | tf_op jit(solution)/shard_map/ppermute | solution.py:760
  61.7 3.2 %combine.8 = (bf16[8,24,3072]{2,1,0:T(8,128)(2,1)S(1)}, bf16[8,24,3072]{2,1,0:T(8,128)(2,1)S(1)}) custom-call(s32[2]{0:T(128)S(1)} %pad_add_fusion.where_ref, bf16[32,24,3072]{2,1,0:T(8,128)(2,1)} %bitcast.36, bf16[32,24,3072]{2,1,0:T(8,128)(2,1)} %collective-permute-done.3.refs_1_.refs_3_.refs_4_.refs_5_.refs_6_.refs_7_, bf16[32,24,3072]{2,1,0:T(8,128)(2,1)} %bitcast.37, ...), custom_call_target="tpu_custom_call" | custom-call | flops 40000000000 | bytes 10000000 | tf_op jit(solution)/shard_map/combine/pallas_call | solution.py:462
  64.9 2.0 %collective-permute-start.5 = (bf16[8,24,3072]{2,1,0:T(8,128)(2,1)S(1)}, bf16[8,24,3072]{2,1,0:T(8,128)(2,1)S(1)}, u32[]{:S(2)}, u32[]{:S(2)}) collective-permute-start(bf16[8,24,3072]{2,1,0:T(8,128)(2,1)S(1)} %get-tuple-element.108), channel_id=1, source_target_pairs={{0,2},{1,3},{2,0},{3,1},{4,6},{5,7},{6,4},{7,5},{8,10},{9,11},{10,... | collective-permute-start | bytes 3538952 | tf_op jit(solution)/shard_map/ppermute | solution.py:551
  66.9 1.5 collective-permute-start.6
  69.5 15.1 %attention.2 = (bf16[768,1024]{1,0:T(8,128)(2,1)}, bf16[768,1024]{1,0:T(8,128)(2,1)}, bf16[4,4,256,128]{3,2,1,0:T(8,128)(2,1)}, bf16[4,4,256,128]{3,2,1,0:T(8,128)(2,1)}) custom-call(s32[2]{0:T(128)} %copy-done.3, s32[4,256]{1,0:T(4,128)} %refs_3_.1, bf16[4,64,3072]{2,1,0:T(8,128)(2,1)} %get-tuple-element.111.q_t_ref, ...), custom_call_target="tpu_custom_call" | custom-call | flops 40000000000 | bytes 10000000 | tf_op jit(solution)/shard_map/attention/pallas_call | solution.py:780
  84.6 8.7 %collective-permute-done.5.refs_2_ = bf16[8,24,3072]{2,1,0:T(8,128)(2,1)S(1)} collective-permute-done((bf16[8,24,3072]{2,1,0:T(8,128)(2,1)S(1)}, bf16[8,24,3072]{2,1,0:T(8,128)(2,1)S(1)}, u32[]{:S(2)}, u32[]{:S(2)}) %collective-permute-start.5) | collective-permute-done | bytes 1179680 | tf_op jit(solution)/shard_map/ppermute | solution.py:551
  93.2 1.6 collective-permute-done.6.refs_5_.refs_6_.refs_7_.refs_8_
  94.8 2.9 %combine.9 = (bf16[4,24,3072]{2,1,0:T(8,128)(2,1)S(1)}, bf16[4,24,3072]{2,1,0:T(8,128)(2,1)S(1)}) custom-call(s32[2]{0:T(128)S(1)} %copy-done.4, bf16[32,24,3072]{2,1,0:T(8,128)(2,1)} %bitcast.38, bf16[32,24,3072]{2,1,0:T(8,128)(2,1)} %collective-permute-done.3.refs_1_.refs_3_.refs_4_.refs_5_.refs_6_.refs_7_, bf16[8,24,3072]{2,1,0:T(8,128)(2,1)} %copy-done.10, ...), custom_call_target="tpu_custom_call" | custom-call | flops 40000000000 | bytes 10000000 | tf_op jit(solution)/shard_map/combine/pallas_call | solution.py:462
  97.7 17.3 %collective-permute-start.7 = (bf16[4,24,3072]{2,1,0:T(8,128)(2,1)S(1)}, bf16[4,24,3072]{2,1,0:T(8,128)(2,1)S(1)}, u32[]{:S(2)}, u32[]{:S(2)}) collective-permute-start(bf16[4,24,3072]{2,1,0:T(8,128)(2,1)S(1)} %get-tuple-element.115), channel_id=1, source_target_pairs={{0,4},{1,5},{2,6},{3,7},{4,0},{5,1},{6,2},{7,3},{8,12},{9,13},{10,... | collective-permute-start | bytes 1769480 | tf_op jit(solution)/shard_map/ppermute | solution.py:551
  115.0 7.2 %attention.3 = (bf16[768,1024]{1,0:T(8,128)(2,1)}, bf16[768,1024]{1,0:T(8,128)(2,1)}, bf16[4,4,256,128]{3,2,1,0:T(8,128)(2,1)}, bf16[4,4,256,128]{3,2,1,0:T(8,128)(2,1)}) custom-call(s32[2]{0:T(128)} %copy-done.3, s32[4,256]{1,0:T(4,128)} %refs_3_.1, ...), custom_call_target="tpu_custom_call", output_to_operand_aliasing={{0}: (8, {}), {1}: (9, {}), {2}: (10, {}), {3}: (11, {})} | custom-call | flops 40000000000 | bytes 10000000 | tf_op jit(solution)/shard_map/attention/pallas_call | solution.py:780
  122.9 2.1 %collective-permute-done.8.refs_7_.refs_8_.refs_9_ = bf16[4,24,3072]{2,1,0:T(8,128)(2,1)S(1)} collective-permute-done((bf16[4,24,3072]{2,1,0:T(8,128)(2,1)S(1)}, bf16[4,24,3072]{2,1,0:T(8,128)(2,1)S(1)}, u32[]{:S(2)}, u32[]{:S(2)}) %collective-permute-start.8) | collective-permute-done | bytes 589856 | tf_op jit(solution)/shard_map/ppermute | solution.py:551
  125.0 2.3 %combine.10 = bf16[2,24,6144]{2,1,0:T(8,128)(2,1)S(1)} custom-call(s32[2]{0:T(128)S(1)} %copy-done.5, bf16[32,24,3072]{2,1,0:T(8,128)(2,1)} %bitcast.40, bf16[32,24,3072]{2,1,0:T(8,128)(2,1)} %collective-permute-done.3.refs_1_.refs_3_.refs_4_.refs_5_.refs_6_.refs_7_, bf16[8,24,3072]{2,1,0:T(8,128)(2,1)} %copy-done.10, ...), custom_call_target="tpu_custom_call" | custom-call | flops 40000000000 | bytes 10000000 | tf_op jit(solution)/shard_map/combine/pallas_call | solution.py:462
  128.1 3.1 %collective-permute-start.11 = (bf16[4,256,128]{2,1,0:T(8,128)(2,1)S(1)}, bf16[4,256,128]{2,1,0:T(8,128)(2,1)S(1)}, u32[]{:S(2)}, u32[]{:S(2)}) collective-permute-start(bf16[4,256,128]{2,1,0:T(8,128)(2,1)S(1)} %get-tuple-element.134), channel_id=1, source_target_pairs={{0,2},{1,3},{2,0},{3,1},{4,6},{5,7},{6,4},{7,5},{8,10},{9,11},{10,... | collective-permute-start | bytes 786440 | tf_op jit(solution)/shard_map/ppermute | solution.py:844
  131.2 5.2 %collective-permute-start.12 = (bf16[4,256,128]{2,1,0:T(8,128)(2,1)S(1)}, bf16[4,256,128]{2,1,0:T(8,128)(2,1)S(1)}, u32[]{:S(2)}, u32[]{:S(2)}) collective-permute-start(bf16[4,256,128]{2,1,0:T(8,128)(2,1)S(1)} %get-tuple-element.135), channel_id=1, source_target_pairs={{0,4},{1,5},{2,6},{3,7},{4,0},{5,1},{6,2},{7,3},{8,12},{9,13},{10,... | collective-permute-start | bytes 786440 | tf_op jit(solution)/shard_map/ppermute | solution.py:844
  136.5 1.4 collective-permute-start.13
  137.9 9.9 %mix.1 = (bf16[4,256,768]{2,1,0:T(8,128)(2,1)}, bf16[2,384,768]{2,1,0:T(8,128)(2,1)}, bf16[2,384,768]{2,1,0:T(8,128)(2,1)}) custom-call(s32[1]{0:T(128)} %bitcast.side_ref.refs_0_, bf16[4,256,768]{2,1,0:T(8,128)(2,1)} %refs_1_.1, s32[4,256]{1,0:T(4,128)} %refs_3_.1, bf16[768,1024]{1,0:T(8,128)(2,1)} %get-tuple-element.121.mix_t_ref, ...), custom_call_target="tpu_custom_call" | custom-call | flops 40000000000 | bytes 10000000 | tf_op jit(solution)/shard_map/mix/pallas_call | solution.py:848
  148.2 1.8 collective-permute-done.13.refs_18_
  150.0 2.0 %combine.11 = bf16[1,24,6144]{2,1,0:T(8,128)(2,1)S(1)} custom-call(s32[2]{0:T(128)S(1)} %copy-done.5, bf16[32,24,3072]{2,1,0:T(8,128)(2,1)} %bitcast.42, bf16[32,24,3072]{2,1,0:T(8,128)(2,1)} %collective-permute-done.3.refs_1_.refs_3_.refs_4_.refs_5_.refs_6_.refs_7_, bf16[8,24,3072]{2,1,0:T(8,128)(2,1)} %copy-done.10, ...), custom_call_target="tpu_custom_call" | custom-call | flops 40000000000 | bytes 10000000 | tf_op jit(solution)/shard_map/combine/pallas_call | solution.py:462
  153.5 1.7 collective-permute-start.16
  155.8 9.4 %exit.1 = (bf16[4,256,768]{2,1,0:T(8,128)(2,1)}, bf16[384,256]{1,0:T(8,128)(2,1)}, bf16[384,256]{1,0:T(8,128)(2,1)}) custom-call(s32[1]{0:T(128)} %bitcast.side_ref.refs_0_, bf16[4,256,768]{2,1,0:T(8,128)(2,1)} %refs_1_.1, bf16[4,256,768]{2,1,0:T(8,128)(2,1)} %refs_2_.1, s32[4,256]{1,0:T(4,128)} %refs_3_.1, ...), custom_call_target="tpu_custom_call" | custom-call | flops 40000000000 | bytes 10000000 | tf_op jit(solution)/shard_map/exit/pallas_call | solution.py:892
  168.0 1.3 collective-permute-start.17
  169.9 1.7 collective-permute-start.22
  172.8 2.7 %own.2 = (f32[24,3072]{1,0:T(8,128)}, f32[24,3072]{1,0:T(8,128)}) custom-call(s32[2]{0:T(128)S(1)} %copy-done.5, bf16[32,24,3072]{2,1,0:T(8,128)(2,1)} %bitcast.44, bf16[32,24,3072]{2,1,0:T(8,128)(2,1)} %collective-permute-done.3.refs_1_.refs_3_.refs_4_.refs_5_.refs_6_.refs_7_, bf16[8,24,3072]{2,1,0:T(8,128)(2,1)} %copy-done.10, ...), custom_call_target="tpu_custom_call" | custom-call | flops 40000000000 | bytes 10000000 | tf_op jit(solution)/shard_map/own/pallas_call | solution.py:462
  177.3 1.3 collective-permute-start.24
  178.6 2.9 %collective-permute-start.25 = (bf16[1,24,1792]{2,1,0:T(8,128)(2,1)S(1)}, bf16[1,24,1792]{2,1,0:T(8,128)(2,1)S(1)}, u32[]{:S(2)}, u32[]{:S(2)}) collective-permute-start(bf16[1,24,1792]{2,1,0:T(8,128)(2,1)S(1)} %get-tuple-element.158), channel_id=1, source_target_pairs={{0,16},{8,24},{16,0},{24,8},{1,17},{9,25},{17,1},{25,9},{2,18},{10... | collective-permute-start | bytes 258056 | tf_op jit(solution)/shard_map/ppermute | solution.py:580
  182.4 3.9 %collective-permute-done.25.refs_5_.refs_12_.refs_20_ = bf16[1,24,1792]{2,1,0:T(8,128)(2,1)S(1)} collective-permute-done((bf16[1,24,1792]{2,1,0:T(8,128)(2,1)S(1)}, bf16[1,24,1792]{2,1,0:T(8,128)(2,1)S(1)}, u32[]{:S(2)}, u32[]{:S(2)}) %collective-permute-start.25) | collective-permute-done | bytes 86048 | tf_op jit(solution)/shard_map/ppermute | solution.py:580
  186.2 1.7 collective-permute-done.26.refs_6_.refs_13_.refs_21_
  (83 shorter events, 18.6 us)
Async XLA Ops:
  1.4 13.6 %copy-start.9 = (bf16[3072]{0:T(1024)(128)(2,1)S(1)}, bf16[3072]{0:T(1024)(128)(2,1)}, u32[]{:S(2)}) copy-start(bf16[3072]{0:T(1024)(128)(2,1)} %param.28) | copy-start | bytes 18436
  10.4 45.9 %collective-permute-start = (bf16[4,272,128]{2,1,0:T(8,128)(2,1)}, bf16[4,272,128]{2,1,0:T(8,128)(2,1)S(1)}, u32[]{:S(2)}, u32[]{:S(2)}) collective-permute-start(bf16[4,272,128]{2,1,0:T(8,128)(2,1)} %get-tuple-element.101.refs_0_), channel_id=1, source_target_pairs={{0,2},{1,3},{2,0},{3,1},{4,6},{5,7},{6,4},{7,5},{8,10},{9,11},{10,... | collective-permute-start | bytes 835592 | tf_op jit(solution)/shard_map/ppermute | solution.py:699
  13.4 42.9 %collective-permute-start.1 = (bf16[4,272,128]{2,1,0:T(8,128)(2,1)}, bf16[4,272,128]{2,1,0:T(8,128)(2,1)S(1)}, u32[]{:S(2)}, u32[]{:S(2)}) collective-permute-start(bf16[4,272,128]{2,1,0:T(8,128)(2,1)} %get-tuple-element.101.refs_0_), channel_id=1, source_target_pairs={{0,4},{1,5},{2,6},{3,7},{4,0},{5,1},{6,2},{7,3},{8,12},{9,13},{10,... | collective-permute-start | bytes 835592 | tf_op jit(solution)/shard_map/ppermute | solution.py:699
  15.0 41.4 %collective-permute-start.2 = (bf16[4,272,128]{2,1,0:T(8,128)(2,1)}, bf16[4,272,128]{2,1,0:T(8,128)(2,1)S(1)}, u32[]{:S(2)}, u32[]{:S(2)}) collective-permute-start(bf16[4,272,128]{2,1,0:T(8,128)(2,1)} %get-tuple-element.101.refs_0_), channel_id=1, source_target_pairs={{0,6},{1,7},{2,4},{3,5},{4,2},{5,3},{6,0},{7,1},{8,14},{9,15},{10,... | collective-permute-start | bytes 835592 | tf_op jit(solution)/shard_map/ppermute | solution.py:699
  15.6 40.7 %copy-start.7 = (bf16[4,272,128]{2,1,0:T(8,128)(2,1)S(1)}, bf16[4,272,128]{2,1,0:T(8,128)(2,1)}, u32[]{:S(2)}) copy-start(bf16[4,272,128]{2,1,0:T(8,128)(2,1)} %get-tuple-element.101.refs_0_) | copy-start | bytes 835588
  53.4 8.3 %collective-permute-start.3 = (bf16[32,24,3072]{2,1,0:T(8,128)(2,1)}, bf16[32,24,3072]{2,1,0:T(8,128)(2,1)}, u32[]{:S(2)}, u32[]{:S(2)}) collective-permute-start(bf16[32,24,3072]{2,1,0:T(8,128)(2,1)} %bitcast.32), channel_id=1, source_target_pairs={{0,1},{1,0},{2,3},{3,2},{4,5},{5,4},{6,7},{7,6},{8,9},{9,8},{10,11... | collective-permute-start | bytes 14155784 | tf_op jit(solution)/shard_map/ppermute | solution.py:760
  56.4 12.0 %collective-permute-start.4 = (bf16[4,4,272,128]{3,2,1,0:T(8,128)(2,1)S(1)}, bf16[4,4,272,128]{3,2,1,0:T(8,128)(2,1)S(1)}, u32[]{:S(2)}, u32[]{:S(2)}) collective-permute-start(bf16[4,4,272,128]{3,2,1,0:T(8,128)(2,1)S(1)} %stack.13.even_ref), channel_id=1, source_target_pairs={{0,1},{1,0},{2,3},{3,2},{4,5},{5,4},{6,7},{7,6},{8,9},{9,8},{10,11... | collective-permute-start | bytes 3342344 | tf_op jit(solution)/shard_map/ppermute | solution.py:751
  64.9 28.3 %collective-permute-start.5 = (bf16[8,24,3072]{2,1,0:T(8,128)(2,1)S(1)}, bf16[8,24,3072]{2,1,0:T(8,128)(2,1)S(1)}, u32[]{:S(2)}, u32[]{:S(2)}) collective-permute-start(bf16[8,24,3072]{2,1,0:T(8,128)(2,1)S(1)} %get-tuple-element.108), channel_id=1, source_target_pairs={{0,2},{1,3},{2,0},{3,1},{4,6},{5,7},{6,4},{7,5},{8,10},{9,11},{10,... | collective-permute-start | bytes 3538952 | tf_op jit(solution)/shard_map/ppermute | solution.py:551
  66.9 27.8 %collective-permute-start.6 = (bf16[8,24,3072]{2,1,0:T(8,128)(2,1)S(1)}, bf16[8,24,3072]{2,1,0:T(8,128)(2,1)}, u32[]{:S(2)}, u32[]{:S(2)}) collective-permute-start(bf16[8,24,3072]{2,1,0:T(8,128)(2,1)S(1)} %get-tuple-element.109), channel_id=1, source_target_pairs={{0,4},{1,5},{2,6},{3,7},{4,0},{5,1},{6,2},{7,3},{8,12},{9,13},{10,... | collective-permute-start | bytes 3538952 | tf_op jit(solution)/shard_map/ppermute | solution.py:551
  69.5 25.3 %copy-start.4 = (s32[2]{0:T(128)S(1)}, s32[2]{0:T(128)}, u32[]{:S(2)}) copy-start(s32[2]{0:T(128)} %copy-done.3) | copy-start | bytes 28
  97.7 25.2 %collective-permute-start.7 = (bf16[4,24,3072]{2,1,0:T(8,128)(2,1)S(1)}, bf16[4,24,3072]{2,1,0:T(8,128)(2,1)S(1)}, u32[]{:S(2)}, u32[]{:S(2)}) collective-permute-start(bf16[4,24,3072]{2,1,0:T(8,128)(2,1)S(1)} %get-tuple-element.115), channel_id=1, source_target_pairs={{0,4},{1,5},{2,6},{3,7},{4,0},{5,1},{6,2},{7,3},{8,12},{9,13},{10,... | collective-permute-start | bytes 1769480 | tf_op jit(solution)/shard_map/ppermute | solution.py:551
  115.0 9.9 %collective-permute-start.8 = (bf16[4,24,3072]{2,1,0:T(8,128)(2,1)S(1)}, bf16[4,24,3072]{2,1,0:T(8,128)(2,1)S(1)}, u32[]{:S(2)}, u32[]{:S(2)}) collective-permute-start(bf16[4,24,3072]{2,1,0:T(8,128)(2,1)S(1)} %get-tuple-element.116), channel_id=1, source_target_pairs={{0,2},{1,3},{2,0},{3,1},{4,6},{5,7},{6,4},{7,5},{8,10},{9,11},{10,... | collective-permute-start | bytes 1769480 | tf_op jit(solution)/shard_map/ppermute | solution.py:551
  115.0 9.9 %copy-start.5 = (s32[2]{0:T(128)S(1)}, s32[2]{0:T(128)}, u32[]{:S(2)}) copy-start(s32[2]{0:T(128)} %copy-done.3) | copy-start | bytes 28
  122.3 5.1 %collective-permute-start.9 = (bf16[4,4,256,128]{3,2,1,0:T(8,128)(2,1)}, bf16[4,4,256,128]{3,2,1,0:T(8,128)(2,1)S(1)}, u32[]{:S(2)}, u32[]{:S(2)}) collective-permute-start(bf16[4,4,256,128]{3,2,1,0:T(8,128)(2,1)} %get-tuple-element.125), channel_id=1, source_target_pairs={{0,1},{1,0},{2,3},{3,2},{4,5},{5,4},{6,7},{7,6},{8,9},{9,8},{10,11... | collective-permute-start | bytes 3145736 | tf_op jit(solution)/shard_map/ppermute | solution.py:828
  127.2 20.6 %collective-permute-start.10 = (bf16[2,24,6144]{2,1,0:T(8,128)(2,1)S(1)}, bf16[2,24,6144]{2,1,0:T(8,128)(2,1)S(1)}, u32[]{:S(2)}, u32[]{:S(2)}) collective-permute-start(bf16[2,24,6144]{2,1,0:T(8,128)(2,1)S(1)} %combine.10), channel_id=1, source_target_pairs={{0,8},{8,0},{16,24},{24,16},{1,9},{9,1},{17,25},{25,17},{2,10},{10... | collective-permute-start | bytes 1769480 | tf_op jit(solution)/shard_map/ppermute | solution.py:551
  128.1 19.6 %copy-start.8 = (bf16[4,256,128]{2,1,0:T(8,128)(2,1)}, bf16[4,256,128]{2,1,0:T(8,128)(2,1)S(1)}, u32[]{:S(2)}) copy-start(bf16[4,256,128]{2,1,0:T(8,128)(2,1)S(1)} %get-tuple-element.126.refs_15_) | copy-start | bytes 786436
  128.1 19.7 %collective-permute-start.11 = (bf16[4,256,128]{2,1,0:T(8,128)(2,1)S(1)}, bf16[4,256,128]{2,1,0:T(8,128)(2,1)S(1)}, u32[]{:S(2)}, u32[]{:S(2)}) collective-permute-start(bf16[4,256,128]{2,1,0:T(8,128)(2,1)S(1)} %get-tuple-element.134), channel_id=1, source_target_pairs={{0,2},{1,3},{2,0},{3,1},{4,6},{5,7},{6,4},{7,5},{8,10},{9,11},{10,... | collective-permute-start | bytes 786440 | tf_op jit(solution)/shard_map/ppermute | solution.py:844
  131.2 17.0 %collective-permute-start.12 = (bf16[4,256,128]{2,1,0:T(8,128)(2,1)S(1)}, bf16[4,256,128]{2,1,0:T(8,128)(2,1)S(1)}, u32[]{:S(2)}, u32[]{:S(2)}) collective-permute-start(bf16[4,256,128]{2,1,0:T(8,128)(2,1)S(1)} %get-tuple-element.135), channel_id=1, source_target_pairs={{0,4},{1,5},{2,6},{3,7},{4,0},{5,1},{6,2},{7,3},{8,12},{9,13},{10,... | collective-permute-start | bytes 786440 | tf_op jit(solution)/shard_map/ppermute | solution.py:844
  136.5 13.5 %collective-permute-start.13 = (bf16[4,256,128]{2,1,0:T(8,128)(2,1)S(1)}, bf16[4,256,128]{2,1,0:T(8,128)(2,1)S(1)}, u32[]{:S(2)}, u32[]{:S(2)}) collective-permute-start(bf16[4,256,128]{2,1,0:T(8,128)(2,1)S(1)} %get-tuple-element.136), channel_id=1, source_target_pairs={{0,6},{1,7},{2,4},{3,5},{4,2},{5,3},{6,0},{7,1},{8,14},{9,15},{10,... | collective-permute-start | bytes 786440 | tf_op jit(solution)/shard_map/ppermute | solution.py:844
  147.7 4.4 %collective-permute-start.14 = (bf16[32,24,768]{2,1,0:T(8,128)(2,1)}, bf16[32,24,768]{2,1,0:T(8,128)(2,1)S(1)}, u32[]{:S(2)}, u32[]{:S(2)}) collective-permute-start(bf16[32,24,768]{2,1,0:T(8,128)(2,1)} %bitcast.33), channel_id=1, source_target_pairs={{0,1},{1,0},{2,3},{3,2},{4,5},{5,4},{6,7},{7,6},{8,9},{9,8},{10,11... | collective-permute-start | bytes 3538952 | tf_op jit(solution)/shard_map/ppermute | solution.py:760
  152.0 19.6 %collective-permute-start.19 = (bf16[1,24,6144]{2,1,0:T(8,128)(2,1)S(1)}, bf16[1,24,6144]{2,1,0:T(8,128)(2,1)S(1)}, u32[]{:S(2)}, u32[]{:S(2)}) collective-permute-start(bf16[1,24,6144]{2,1,0:T(8,128)(2,1)S(1)} %combine.11), channel_id=1, source_target_pairs={{0,16},{8,24},{16,0},{24,8},{1,17},{9,25},{17,1},{25,9},{2,18},{10... | collective-permute-start | bytes 884744 | tf_op jit(solution)/shard_map/ppermute | solution.py:551
  152.8 12.5 %collective-permute-start.15 = (bf16[8,24,768]{2,1,0:T(8,128)(2,1)S(1)}, bf16[8,24,768]{2,1,0:T(8,128)(2,1)S(1)}, u32[]{:S(2)}, u32[]{:S(2)}) collective-permute-start(bf16[8,24,768]{2,1,0:T(8,128)(2,1)S(1)} %get-tuple-element.140), channel_id=1, source_target_pairs={{0,2},{1,3},{2,0},{3,1},{4,6},{5,7},{6,4},{7,5},{8,10},{9,11},{10,... | collective-permute-start | bytes 884744 | tf_op jit(solution)/shard_map/ppermute | solution.py:551
  153.5 11.8 %collective-permute-start.16 = (bf16[8,24,768]{2,1,0:T(8,128)(2,1)S(1)}, bf16[8,24,768]{2,1,0:T(8,128)(2,1)S(1)}, u32[]{:S(2)}, u32[]{:S(2)}) collective-permute-start(bf16[8,24,768]{2,1,0:T(8,128)(2,1)S(1)} %get-tuple-element.141), channel_id=1, source_target_pairs={{0,4},{1,5},{2,6},{3,7},{4,0},{5,1},{6,2},{7,3},{8,12},{9,13},{10,... | collective-permute-start | bytes 884744 | tf_op jit(solution)/shard_map/ppermute | solution.py:551
  165.2 1.7 collective-permute-start.18
  167.5 8.0 %collective-permute-start.21 = (bf16[4,24,256]{2,1,0:T(8,128)(2,1)S(1)}, bf16[4,24,256]{2,1,0:T(8,128)(2,1)S(1)}, u32[]{:S(2)}, u32[]{:S(2)}) collective-permute-start(bf16[4,24,256]{2,1,0:T(8,128)(2,1)S(1)} %get-tuple-element.151), channel_id=1, source_target_pairs={{0,2},{1,3},{2,0},{3,1},{4,6},{5,7},{6,4},{7,5},{8,10},{9,11},{10,... | collective-permute-start | bytes 147464 | tf_op jit(solution)/shard_map/ppermute | solution.py:580
  168.0 8.6 %collective-permute-start.17 = (bf16[4,24,768]{2,1,0:T(8,128)(2,1)S(1)}, bf16[4,24,768]{2,1,0:T(8,128)(2,1)S(1)}, u32[]{:S(2)}, u32[]{:S(2)}) collective-permute-start(bf16[4,24,768]{2,1,0:T(8,128)(2,1)S(1)} %get-tuple-element.147), channel_id=1, source_target_pairs={{0,4},{1,5},{2,6},{3,7},{4,0},{5,1},{6,2},{7,3},{8,12},{9,13},{10,... | collective-permute-start | bytes 442376 | tf_op jit(solution)/shard_map/ppermute | solution.py:551
  169.3 7.3 %collective-permute-start.20 = (bf16[4,24,768]{2,1,0:T(8,128)(2,1)S(1)}, bf16[4,24,768]{2,1,0:T(8,128)(2,1)S(1)}, u32[]{:S(2)}, u32[]{:S(2)}) collective-permute-start(bf16[4,24,768]{2,1,0:T(8,128)(2,1)S(1)} %get-tuple-element.148), channel_id=1, source_target_pairs={{0,2},{1,3},{2,0},{3,1},{4,6},{5,7},{6,4},{7,5},{8,10},{9,11},{10,... | collective-permute-start | bytes 442376 | tf_op jit(solution)/shard_map/ppermute | solution.py:551
  169.9 5.7 %collective-permute-start.22 = (bf16[4,24,256]{2,1,0:T(8,128)(2,1)S(1)}, bf16[4,24,256]{2,1,0:T(8,128)(2,1)S(1)}, u32[]{:S(2)}, u32[]{:S(2)}) collective-permute-start(bf16[4,24,256]{2,1,0:T(8,128)(2,1)S(1)} %get-tuple-element.155), channel_id=1, source_target_pairs={{0,4},{1,5},{2,6},{3,7},{4,0},{5,1},{6,2},{7,3},{8,12},{9,13},{10,... | collective-permute-start | bytes 147464 | tf_op jit(solution)/shard_map/ppermute | solution.py:580
  171.6 5.0 %collective-permute-start.23 = (bf16[4,24,256]{2,1,0:T(8,128)(2,1)S(1)}, bf16[4,24,256]{2,1,0:T(8,128)(2,1)S(1)}, u32[]{:S(2)}, u32[]{:S(2)}) collective-permute-start(bf16[4,24,256]{2,1,0:T(8,128)(2,1)S(1)} %get-tuple-element.156), channel_id=1, source_target_pairs={{0,6},{1,7},{2,4},{3,5},{4,2},{5,3},{6,0},{7,1},{8,14},{9,15},{10,... | collective-permute-start | bytes 147464 | tf_op jit(solution)/shard_map/ppermute | solution.py:580
  177.3 5.0 %collective-permute-start.24 = (bf16[1,24,1792]{2,1,0:T(8,128)(2,1)S(1)}, bf16[1,24,1792]{2,1,0:T(8,128)(2,1)S(1)}, u32[]{:S(2)}, u32[]{:S(2)}) collective-permute-start(bf16[1,24,1792]{2,1,0:T(8,128)(2,1)S(1)} %get-tuple-element.157), channel_id=1, source_target_pairs={{0,8},{8,0},{16,24},{24,16},{1,9},{9,1},{17,25},{25,17},{2,10},{10... | collective-permute-start | bytes 258056 | tf_op jit(solution)/shard_map/ppermute | solution.py:580
  178.6 7.6 %collective-permute-start.25 = (bf16[1,24,1792]{2,1,0:T(8,128)(2,1)S(1)}, bf16[1,24,1792]{2,1,0:T(8,128)(2,1)S(1)}, u32[]{:S(2)}, u32[]{:S(2)}) collective-permute-start(bf16[1,24,1792]{2,1,0:T(8,128)(2,1)S(1)} %get-tuple-element.158), channel_id=1, source_target_pairs={{0,16},{8,24},{16,0},{24,8},{1,17},{9,25},{17,1},{25,9},{2,18},{10... | collective-permute-start | bytes 258056 | tf_op jit(solution)/shard_map/ppermute | solution.py:580
  181.5 6.4 %collective-permute-start.26 = (bf16[1,24,1792]{2,1,0:T(8,128)(2,1)S(1)}, bf16[1,24,1792]{2,1,0:T(8,128)(2,1)S(1)}, u32[]{:S(2)}, u32[]{:S(2)}) collective-permute-start(bf16[1,24,1792]{2,1,0:T(8,128)(2,1)S(1)} %get-tuple-element.159), channel_id=1, source_target_pairs={{0,24},{8,16},{16,8},{24,0},{1,25},{9,17},{17,9},{25,1},{2,26},{10... | collective-permute-start | bytes 258056 | tf_op jit(solution)/shard_map/ppermute | solution.py:580
  (10 other events, 35.3 us)
where the time goes:
time: 190 us; the launch traced here: 191 us
  Pallas kernels  106 us (56%)
  starting transfers between devices  48.2 us (25%)
  waiting for transfers between devices  28 us (15%)
  local copies, waits for them, and re-layouts  4.76 us (3%)
  other arithmetic  2.78 us (1%)
    pallas_call x1, Pallas kernels, on_device(): pl.pallas_call(functools.partial(mlp_kernel, token_count), grid_spec=pltp...  37.8 us
    ppermute x10, starting transfers between devices, reduce_level(): lax.ppermute(send, AXES[axis], partners(lax.axis_size(AXES[axis]), 1 << b...  25.2 us
    pallas_call x2, Pallas kernels, attention(): pl.pallas_call(functools.partial(attention_kernel, heads, head_size, seq_...  22.3 us
    pallas_call x11, Pallas kernels, call_on_terms(): pl.pallas_call(body, grid_spec=pltpu.PrefetchScalarGridSpec(num_scalar_pr...  17.8 us
    ppermute x10, waiting for transfers between devices, reduce_level(): lax.ppermute(send, AXES[axis], partners(lax.axis_size(AXES[axis]), 1 << b...  12.9 us
    pallas_call x1, Pallas kernels, on_device(): pl.pallas_call(mix_kernel, grid_spec=pltpu.PrefetchScalarGridSpec(num_sca...  9.86 us
    ppermute x3, starting transfers between devices, on_device(): lax.ppermute(shares[j], 'seq', partners(seq_devices, 2 * j))  9.73 us
    pallas_call x1, Pallas kernels, on_device(): pl.pallas_call(exit_body, grid_spec=pltpu.PrefetchScalarGridSpec(num_scal...  9.38 us
  transfers between devices with their start and end apart: 27, of which 12 were waited for; matrix products, arithmetic and copies ran while one was open for 2% of the time, Pallas kernels for 48%

commit v1 on v0

--- a/solution.py
+++ b/solution.py
@@ -508,7 +508,7 @@
     shapes = [(stream.rows, stream.width) for stream in streams]
     if vectors:
         shapes[-1] = (shapes[-1][0], shapes[-1][1] - LANES)
-        shapes += [(streams[-1].rows,)] * len(vectors)
+        shapes += [(streams[-1].rows * len(columns),) for columns in vectors]
 
     def body(where_ref, *refs):
         at = 0
@@ -519,8 +519,9 @@
             at += size
         if vectors:
             turned = total[:, -LANES:].T
-            for row, output in zip(vectors, refs[len(terms) + len(streams) :]):
-                output[...] = turned[row : row + 1].reshape(output.shape)
+            for columns, output in zip(vectors, refs[len(terms) + len(streams) :]):
+                row = jnp.concatenate([turned[c : c + 1] for c in columns], axis=1)
+                output[...] = row.reshape(output.shape)
 
     return call_on_terms(
         body, "own", where, after, 1,
@@ -880,7 +881,7 @@
         exit_kernel(order_a, rows, permuted, *fixed, rest[:dkv_count], *rest[dkv_count:])
 
     if permuted:
-        shuffle = jnp.zeros((8, LANES), F32)
+        shuffle = cosine
     else:
         places = (jnp.array(order_a)[:, None] * rows + jnp.arange(rows)[None, :]).reshape(width, 1)
         shuffle = (places == jnp.arange(width)[None, :]).astype(F32)
@@ -931,8 +932,8 @@
     sums = own_sums(mlp_streams, where, after, LONG)
     small_streams = mix_streams + extra_streams
     exchange(small_streams, batch_bits, where, sums[:1])
-    several = hidden // width
-    sums += own_sums(small_streams, where, vectors=[*range(6), *range(8, 8 + several)])
+    several = tuple(range(8, 8 + hidden // width))
+    sums += own_sums(small_streams, where, vectors=[(0,), (1,), (2,), (3,), (4,), (5,), (5,), several])
     w_up_grad, w_down_grad_t, w_query_grad, w_out_grad_t, w_keyvalue_grad, *vectors = sums
     return (
         output,
@@ -948,9 +949,9 @@
         w_out_grad_t.T,
         vectors[5],
         w_up_grad,
-        jnp.concatenate(vectors[6:]),
+        vectors[7],
         w_down_grad_t.T,
-        vectors[5],
+        vectors[6],
     )
 
 

time: 190 us -> 188 us (0.989)
    ppermute x1, starting transfers between devices: 0.01 us -> 2.62 us  [on_device(): dkv_recv = lax.ppermute(dkv_send, 'seq', partners(seq_devices, 1))]
    ppermute x3, starting transfers between devices: 9.73 us -> 7.72 us  [on_device(): lax.ppermute(shares[j], 'seq', partners(seq_devices, 2 * j))]
  transfers between devices with their start and end apart: 27 -> 27, of which waited for: 12 -> 9; matrix products, arithmetic and copies ran while one was open for 2% -> 2% of each run, Pallas kernels for 48% -> 50%
where the time goes in v1:
time: 188 us; the launch traced here: 187 us
  Pallas kernels  107 us (57%)
  starting transfers between devices  47 us (25%)
  waiting for transfers between devices  27.1 us (14%)
  local copies, waits for them, and re-layouts  3 us (2%)
  other arithmetic  2.19 us (1%)
    pallas_call x1, Pallas kernels, on_device(): pl.pallas_call(functools.partial(mlp_kernel, token_count), grid_spec=pltp...  37.9 us
    ppermute x10, starting transfers between devices, reduce_level(): lax.ppermute(send, AXES[axis], partners(lax.axis_size(AXES[axis]), 1 << b...  23.4 us
    pallas_call x2, Pallas kernels, attention(): pl.pallas_call(functools.partial(attention_kernel, heads, head_size, seq_...  22.6 us
    pallas_call x11, Pallas kernels, call_on_terms(): pl.pallas_call(body, grid_spec=pltpu.PrefetchScalarGridSpec(num_scalar_pr...  17.9 us
    ppermute x10, waiting for transfers between devices, reduce_level(): lax.ppermute(send, AXES[axis], partners(lax.axis_size(AXES[axis]), 1 << b...  13.1 us
    pallas_call x1, Pallas kernels, on_device(): pl.pallas_call(mix_kernel, grid_spec=pltpu.PrefetchScalarGridSpec(num_sca...  9.85 us
    pallas_call x1, Pallas kernels, on_device(): pl.pallas_call(exit_body, grid_spec=pltpu.PrefetchScalarGridSpec(num_scal...  9.56 us
    pallas_call x1, Pallas kernels, on_device(): pl.pallas_call(functools.partial(entry_kernel, head_size, order_a, order_...  9.04 us
  transfers between devices with their start and end apart: 27, of which 9 were waited for; matrix products, arithmetic and copies ran while one was open for 2% of the time, Pallas kernels for 50%

profile of v1, /device:TPU:0, one launch (start us, length us, event | category | flops | bytes accessed | tf_op | source)
XLA Modules:
  0.0 187.3 jit_solution(14830865828111390988)
XLA Ops:
  1.4 9.0 %entry.1 = (bf16[1024,768]{1,0:T(8,128)(2,1)}, bf16[1024,768]{1,0:T(8,128)(2,1)}, bf16[768,1024]{1,0:T(8,128)(2,1)}, bf16[768,1024]{1,0:T(8,128)(2,1)}, bf16[768...) custom-call(bf16[4,256,768]{2,1,0:T(8,128)(2,1)} %refs_1_.1, ...), custom_call_target="tpu_custom_call" | custom-call | flops 40000000000 | bytes 10000000 | tf_op jit(solution)/shard_map/entry/pallas_call | solution.py:663
  10.4 4.0 %collective-permute-start.2 = (bf16[4,272,128]{2,1,0:T(8,128)(2,1)}, bf16[4,272,128]{2,1,0:T(8,128)(2,1)S(1)}, u32[]{:S(2)}, u32[]{:S(2)}) collective-permute-start(bf16[4,272,128]{2,1,0:T(8,128)(2,1)} %get-tuple-element.99.refs_0_), channel_id=1, source_target_pairs={{0,6},{1,7},{2,4},{3,5},{4,2},{5,3},{6,0},{7,1},{8,14},{9,15},{10,... | collective-permute-start | bytes 835592 | tf_op jit(solution)/shard_map/ppermute | solution.py:700
  15.7 37.9 %mlp.1 = (bf16[2,384,3072]{2,1,0:T(8,128)(2,1)}, bf16[2,384,3072]{2,1,0:T(8,128)(2,1)}, f32[1024,768]{1,0:T(8,128)}, f32[1024,768]{1,0:T(8,128)}, f32[1,3072]{1,0:T(1,128)}) custom-call(s32[1]{0:T(128)} %bitcast.side_ref.refs_0_, bf16[1024,768]{1,0:T(8,128)(2,1)} %get-tuple-element.94.mlp_ref, bf16[1024,768]{1,0:T(8,128)(2,1)} %get-tuple-element.95.bg_ref, ...), custom_call_target="tpu_custom_call" | custom-call | flops 40000000000 | bytes 10000000 | tf_op jit(solution)/shard_map/mlp/pallas_call | solution.py:706
  54.2 1.4 reduce.3
  57.2 4.7 %collective-permute-done.3.refs_1_.refs_3_.refs_4_.refs_5_.refs_6_.refs_7_ = bf16[32,24,3072]{2,1,0:T(8,128)(2,1)} collective-permute-done((bf16[32,24,3072]{2,1,0:T(8,128)(2,1)}, bf16[32,24,3072]{2,1,0:T(8,128)(2,1)}, u32[]{:S(2)}, u32[]{:S(2)}) %collective-permute-start.3) | collective-permute-done | bytes 4718624 | tf_op jit(solution)/shard_map/ppermute | solution.py:761
  61.9 3.2 %combine.8 = (bf16[8,24,3072]{2,1,0:T(8,128)(2,1)S(1)}, bf16[8,24,3072]{2,1,0:T(8,128)(2,1)S(1)}) custom-call(s32[2]{0:T(128)S(1)} %pad_add_fusion.where_ref, bf16[32,24,3072]{2,1,0:T(8,128)(2,1)} %bitcast.36, bf16[32,24,3072]{2,1,0:T(8,128)(2,1)} %collective-permute-done.3.refs_1_.refs_3_.refs_4_.refs_5_.refs_6_.refs_7_, bf16[32,24,3072]{2,1,0:T(8,128)(2,1)} %bitcast.37, ...), custom_call_target="tpu_custom_call" | custom-call | flops 40000000000 | bytes 10000000 | tf_op jit(solution)/shard_map/combine/pallas_call | solution.py:462
  65.1 2.0 %collective-permute-start.5 = (bf16[8,24,3072]{2,1,0:T(8,128)(2,1)S(1)}, bf16[8,24,3072]{2,1,0:T(8,128)(2,1)S(1)}, u32[]{:S(2)}, u32[]{:S(2)}) collective-permute-start(bf16[8,24,3072]{2,1,0:T(8,128)(2,1)S(1)} %get-tuple-element.106), channel_id=1, source_target_pairs={{0,2},{1,3},{2,0},{3,1},{4,6},{5,7},{6,4},{7,5},{8,10},{9,11},{10,... | collective-permute-start | bytes 3538952 | tf_op jit(solution)/shard_map/ppermute | solution.py:552
  67.1 1.5 collective-permute-start.6
  69.6 15.4 %attention.2 = (bf16[768,1024]{1,0:T(8,128)(2,1)}, bf16[768,1024]{1,0:T(8,128)(2,1)}, bf16[4,4,256,128]{3,2,1,0:T(8,128)(2,1)}, bf16[4,4,256,128]{3,2,1,0:T(8,128)(2,1)}) custom-call(s32[2]{0:T(128)} %copy-done.3, s32[4,256]{1,0:T(4,128)} %refs_3_.1, bf16[4,64,3072]{2,1,0:T(8,128)(2,1)} %get-tuple-element.109.q_t_ref, ...), custom_call_target="tpu_custom_call" | custom-call | flops 40000000000 | bytes 10000000 | tf_op jit(solution)/shard_map/attention/pallas_call | solution.py:781
  84.9 8.4 %collective-permute-done.5.refs_2_ = bf16[8,24,3072]{2,1,0:T(8,128)(2,1)S(1)} collective-permute-done((bf16[8,24,3072]{2,1,0:T(8,128)(2,1)S(1)}, bf16[8,24,3072]{2,1,0:T(8,128)(2,1)S(1)}, u32[]{:S(2)}, u32[]{:S(2)}) %collective-permute-start.5) | collective-permute-done | bytes 1179680 | tf_op jit(solution)/shard_map/ppermute | solution.py:552
  93.3 1.6 collective-permute-done.6.refs_5_.refs_6_.refs_7_.refs_8_
  94.9 2.9 %combine.9 = (bf16[4,24,3072]{2,1,0:T(8,128)(2,1)S(1)}, bf16[4,24,3072]{2,1,0:T(8,128)(2,1)S(1)}) custom-call(s32[2]{0:T(128)S(1)} %copy-done.4, bf16[32,24,3072]{2,1,0:T(8,128)(2,1)} %bitcast.38, bf16[32,24,3072]{2,1,0:T(8,128)(2,1)} %collective-permute-done.3.refs_1_.refs_3_.refs_4_.refs_5_.refs_6_.refs_7_, bf16[8,24,3072]{2,1,0:T(8,128)(2,1)} %copy-done.10, ...), custom_call_target="tpu_custom_call" | custom-call | flops 40000000000 | bytes 10000000 | tf_op jit(solution)/shard_map/combine/pallas_call | solution.py:462
  97.8 1.7 collective-permute-start.7
  99.5 6.8 %collective-permute-start.8 = (bf16[4,24,3072]{2,1,0:T(8,128)(2,1)S(1)}, bf16[4,24,3072]{2,1,0:T(8,128)(2,1)S(1)}, u32[]{:S(2)}, u32[]{:S(2)}) collective-permute-start(bf16[4,24,3072]{2,1,0:T(8,128)(2,1)S(1)} %get-tuple-element.114), channel_id=1, source_target_pairs={{0,2},{1,3},{2,0},{3,1},{4,6},{5,7},{6,4},{7,5},{8,10},{9,11},{10,... | collective-permute-start | bytes 1769480 | tf_op jit(solution)/shard_map/ppermute | solution.py:552
  106.3 7.3 %attention.3 = (bf16[768,1024]{1,0:T(8,128)(2,1)}, bf16[768,1024]{1,0:T(8,128)(2,1)}, bf16[4,4,256,128]{3,2,1,0:T(8,128)(2,1)}, bf16[4,4,256,128]{3,2,1,0:T(8,128)(2,1)}) custom-call(s32[2]{0:T(128)} %copy-done.3, s32[4,256]{1,0:T(4,128)} %refs_3_.1, ...), custom_call_target="tpu_custom_call", output_to_operand_aliasing={{0}: (8, {}), {1}: (9, {}), {2}: (10, {}), {3}: (11, {})} | custom-call | flops 40000000000 | bytes 10000000 | tf_op jit(solution)/shard_map/attention/pallas_call | solution.py:781
  113.6 2.6 %collective-permute-start.9 = (bf16[4,4,256,128]{3,2,1,0:T(8,128)(2,1)}, bf16[4,4,256,128]{3,2,1,0:T(8,128)(2,1)S(1)}, u32[]{:S(2)}, u32[]{:S(2)}) collective-permute-start(bf16[4,4,256,128]{3,2,1,0:T(8,128)(2,1)} %get-tuple-element.123), channel_id=1, source_target_pairs={{0,1},{1,0},{2,3},{3,2},{4,5},{5,4},{6,7},{7,6},{8,9},{9,8},{10,11... | collective-permute-start | bytes 3145736 | tf_op jit(solution)/shard_map/ppermute | solution.py:829
  116.2 3.2 %collective-permute-done.8.refs_7_.refs_8_.refs_9_ = bf16[4,24,3072]{2,1,0:T(8,128)(2,1)S(1)} collective-permute-done((bf16[4,24,3072]{2,1,0:T(8,128)(2,1)S(1)}, bf16[4,24,3072]{2,1,0:T(8,128)(2,1)S(1)}, u32[]{:S(2)}, u32[]{:S(2)}) %collective-permute-start.8) | collective-permute-done | bytes 589856 | tf_op jit(solution)/shard_map/ppermute | solution.py:552
  119.3 2.3 %combine.10 = bf16[2,24,6144]{2,1,0:T(8,128)(2,1)S(1)} custom-call(s32[2]{0:T(128)S(1)} %copy-done.5, bf16[32,24,3072]{2,1,0:T(8,128)(2,1)} %bitcast.40, bf16[32,24,3072]{2,1,0:T(8,128)(2,1)} %collective-permute-done.3.refs_1_.refs_3_.refs_4_.refs_5_.refs_6_.refs_7_, bf16[8,24,3072]{2,1,0:T(8,128)(2,1)} %copy-done.10, ...), custom_call_target="tpu_custom_call" | custom-call | flops 40000000000 | bytes 10000000 | tf_op jit(solution)/shard_map/combine/pallas_call | solution.py:462
  121.6 1.7 collective-permute-start.10
  124.1 6.2 %collective-permute-start.11 = (bf16[4,256,128]{2,1,0:T(8,128)(2,1)S(1)}, bf16[4,256,128]{2,1,0:T(8,128)(2,1)S(1)}, u32[]{:S(2)}, u32[]{:S(2)}) collective-permute-start(bf16[4,256,128]{2,1,0:T(8,128)(2,1)S(1)} %get-tuple-element.132), channel_id=1, source_target_pairs={{0,2},{1,3},{2,0},{3,1},{4,6},{5,7},{6,4},{7,5},{8,10},{9,11},{10,... | collective-permute-start | bytes 786440 | tf_op jit(solution)/shard_map/ppermute | solution.py:845
  130.4 1.5 collective-permute-start.13
  131.8 9.9 %mix.1 = (bf16[4,256,768]{2,1,0:T(8,128)(2,1)}, bf16[2,384,768]{2,1,0:T(8,128)(2,1)}, bf16[2,384,768]{2,1,0:T(8,128)(2,1)}) custom-call(s32[1]{0:T(128)} %bitcast.side_ref.refs_0_, bf16[4,256,768]{2,1,0:T(8,128)(2,1)} %refs_1_.1, s32[4,256]{1,0:T(4,128)} %refs_3_.1, bf16[768,1024]{1,0:T(8,128)(2,1)} %get-tuple-element.119.mix_t_ref, ...), custom_call_target="tpu_custom_call" | custom-call | flops 40000000000 | bytes 10000000 | tf_op jit(solution)/shard_map/mix/pallas_call | solution.py:849
  141.8 2.2 %collective-permute-done.12.refs_17_ = bf16[4,256,128]{2,1,0:T(8,128)(2,1)S(1)} collective-permute-done((bf16[4,256,128]{2,1,0:T(8,128)(2,1)S(1)}, bf16[4,256,128]{2,1,0:T(8,128)(2,1)S(1)}, u32[]{:S(2)}, u32[]{:S(2)}) %collective-permute-start.12) | collective-permute-done | bytes 262176 | tf_op jit(solution)/shard_map/ppermute | solution.py:845
  144.0 2.0 %combine.11 = bf16[1,24,6144]{2,1,0:T(8,128)(2,1)S(1)} custom-call(s32[2]{0:T(128)S(1)} %copy-done.5, bf16[32,24,3072]{2,1,0:T(8,128)(2,1)} %bitcast.42, bf16[32,24,3072]{2,1,0:T(8,128)(2,1)} %collective-permute-done.3.refs_1_.refs_3_.refs_4_.refs_5_.refs_6_.refs_7_, bf16[8,24,3072]{2,1,0:T(8,128)(2,1)} %copy-done.10, ...), custom_call_target="tpu_custom_call" | custom-call | flops 40000000000 | bytes 10000000 | tf_op jit(solution)/shard_map/combine/pallas_call | solution.py:462
  146.1 5.6 %collective-permute-start.19 = (bf16[1,24,6144]{2,1,0:T(8,128)(2,1)S(1)}, bf16[1,24,6144]{2,1,0:T(8,128)(2,1)S(1)}, u32[]{:S(2)}, u32[]{:S(2)}) collective-permute-start(bf16[1,24,6144]{2,1,0:T(8,128)(2,1)S(1)} %combine.11), channel_id=1, source_target_pairs={{0,16},{8,24},{16,0},{24,8},{1,17},{9,25},{17,1},{25,9},{2,18},{10... | collective-permute-start | bytes 884744 | tf_op jit(solution)/shard_map/ppermute | solution.py:552
  153.0 1.7 collective-permute-start.16
  154.8 9.6 %exit.1 = (bf16[4,256,768]{2,1,0:T(8,128)(2,1)}, bf16[384,256]{1,0:T(8,128)(2,1)}, bf16[384,256]{1,0:T(8,128)(2,1)}) custom-call(s32[1]{0:T(128)} %bitcast.side_ref.refs_0_, bf16[4,256,768]{2,1,0:T(8,128)(2,1)} %refs_1_.1, bf16[4,256,768]{2,1,0:T(8,128)(2,1)} %refs_2_.1, s32[4,256]{1,0:T(4,128)} %refs_3_.1, ...), custom_call_target="tpu_custom_call" | custom-call | flops 40000000000 | bytes 10000000 | tf_op jit(solution)/shard_map/exit/pallas_call | solution.py:893
  169.0 1.7 collective-permute-start.22
  171.9 2.7 %own.2 = (f32[24,3072]{1,0:T(8,128)}, f32[24,3072]{1,0:T(8,128)}) custom-call(s32[2]{0:T(128)S(1)} %copy-done.5, bf16[32,24,3072]{2,1,0:T(8,128)(2,1)} %bitcast.44, bf16[32,24,3072]{2,1,0:T(8,128)(2,1)} %collective-permute-done.3.refs_1_.refs_3_.refs_4_.refs_5_.refs_6_.refs_7_, bf16[8,24,3072]{2,1,0:T(8,128)(2,1)} %copy-done.10, ...), custom_call_target="tpu_custom_call" | custom-call | flops 40000000000 | bytes 10000000 | tf_op jit(solution)/shard_map/own/pallas_call | solution.py:462
  177.9 3.1 %collective-permute-start.26 = (bf16[1,24,1792]{2,1,0:T(8,128)(2,1)S(1)}, bf16[1,24,1792]{2,1,0:T(8,128)(2,1)S(1)}, u32[]{:S(2)}, u32[]{:S(2)}) collective-permute-start(bf16[1,24,1792]{2,1,0:T(8,128)(2,1)S(1)} %get-tuple-element.157), channel_id=1, source_target_pairs={{0,24},{8,16},{16,8},{24,0},{1,25},{9,17},{17,9},{25,1},{2,26},{10... | collective-permute-start | bytes 258056 | tf_op jit(solution)/shard_map/ppermute | solution.py:581
  181.6 4.4 %collective-permute-done.25.refs_5_.refs_12_.refs_20_ = bf16[1,24,1792]{2,1,0:T(8,128)(2,1)S(1)} collective-permute-done((bf16[1,24,1792]{2,1,0:T(8,128)(2,1)S(1)}, bf16[1,24,1792]{2,1,0:T(8,128)(2,1)S(1)}, u32[]{:S(2)}, u32[]{:S(2)}) %collective-permute-start.25) | collective-permute-done | bytes 86048 | tf_op jit(solution)/shard_map/ppermute | solution.py:581
  185.9 1.3 own.3
  (80 shorter events, 17.0 us)
Async XLA Ops:
  1.4 13.6 %copy-start.9 = (bf16[3072]{0:T(1024)(128)(2,1)S(1)}, bf16[3072]{0:T(1024)(128)(2,1)}, u32[]{:S(2)}) copy-start(bf16[3072]{0:T(1024)(128)(2,1)} %param.28) | copy-start | bytes 18436
  10.4 46.0 %collective-permute-start.2 = (bf16[4,272,128]{2,1,0:T(8,128)(2,1)}, bf16[4,272,128]{2,1,0:T(8,128)(2,1)S(1)}, u32[]{:S(2)}, u32[]{:S(2)}) collective-permute-start(bf16[4,272,128]{2,1,0:T(8,128)(2,1)} %get-tuple-element.99.refs_0_), channel_id=1, source_target_pairs={{0,6},{1,7},{2,4},{3,5},{4,2},{5,3},{6,0},{7,1},{8,14},{9,15},{10,... | collective-permute-start | bytes 835592 | tf_op jit(solution)/shard_map/ppermute | solution.py:700
  14.4 42.1 %collective-permute-start.1 = (bf16[4,272,128]{2,1,0:T(8,128)(2,1)}, bf16[4,272,128]{2,1,0:T(8,128)(2,1)S(1)}, u32[]{:S(2)}, u32[]{:S(2)}) collective-permute-start(bf16[4,272,128]{2,1,0:T(8,128)(2,1)} %get-tuple-element.99.refs_0_), channel_id=1, source_target_pairs={{0,4},{1,5},{2,6},{3,7},{4,0},{5,1},{6,2},{7,3},{8,12},{9,13},{10,... | collective-permute-start | bytes 835592 | tf_op jit(solution)/shard_map/ppermute | solution.py:700
  14.9 41.6 %collective-permute-start = (bf16[4,272,128]{2,1,0:T(8,128)(2,1)}, bf16[4,272,128]{2,1,0:T(8,128)(2,1)S(1)}, u32[]{:S(2)}, u32[]{:S(2)}) collective-permute-start(bf16[4,272,128]{2,1,0:T(8,128)(2,1)} %get-tuple-element.99.refs_0_), channel_id=1, source_target_pairs={{0,2},{1,3},{2,0},{3,1},{4,6},{5,7},{6,4},{7,5},{8,10},{9,11},{10,... | collective-permute-start | bytes 835592 | tf_op jit(solution)/shard_map/ppermute | solution.py:700
  15.6 40.8 %copy-start.7 = (bf16[4,272,128]{2,1,0:T(8,128)(2,1)S(1)}, bf16[4,272,128]{2,1,0:T(8,128)(2,1)}, u32[]{:S(2)}) copy-start(bf16[4,272,128]{2,1,0:T(8,128)(2,1)} %get-tuple-element.99.refs_0_) | copy-start | bytes 835588
  53.6 8.3 %collective-permute-start.3 = (bf16[32,24,3072]{2,1,0:T(8,128)(2,1)}, bf16[32,24,3072]{2,1,0:T(8,128)(2,1)}, u32[]{:S(2)}, u32[]{:S(2)}) collective-permute-start(bf16[32,24,3072]{2,1,0:T(8,128)(2,1)} %bitcast.32), channel_id=1, source_target_pairs={{0,1},{1,0},{2,3},{3,2},{4,5},{5,4},{6,7},{7,6},{8,9},{9,8},{10,11... | collective-permute-start | bytes 14155784 | tf_op jit(solution)/shard_map/ppermute | solution.py:761
  56.6 12.0 %collective-permute-start.4 = (bf16[4,4,272,128]{3,2,1,0:T(8,128)(2,1)S(1)}, bf16[4,4,272,128]{3,2,1,0:T(8,128)(2,1)S(1)}, u32[]{:S(2)}, u32[]{:S(2)}) collective-permute-start(bf16[4,4,272,128]{3,2,1,0:T(8,128)(2,1)S(1)} %stack.13.even_ref), channel_id=1, source_target_pairs={{0,1},{1,0},{2,3},{3,2},{4,5},{5,4},{6,7},{7,6},{8,9},{9,8},{10,11... | collective-permute-start | bytes 3342344 | tf_op jit(solution)/shard_map/ppermute | solution.py:752
  65.1 28.2 %collective-permute-start.5 = (bf16[8,24,3072]{2,1,0:T(8,128)(2,1)S(1)}, bf16[8,24,3072]{2,1,0:T(8,128)(2,1)S(1)}, u32[]{:S(2)}, u32[]{:S(2)}) collective-permute-start(bf16[8,24,3072]{2,1,0:T(8,128)(2,1)S(1)} %get-tuple-element.106), channel_id=1, source_target_pairs={{0,2},{1,3},{2,0},{3,1},{4,6},{5,7},{6,4},{7,5},{8,10},{9,11},{10,... | collective-permute-start | bytes 3538952 | tf_op jit(solution)/shard_map/ppermute | solution.py:552
  67.1 27.8 %collective-permute-start.6 = (bf16[8,24,3072]{2,1,0:T(8,128)(2,1)S(1)}, bf16[8,24,3072]{2,1,0:T(8,128)(2,1)}, u32[]{:S(2)}, u32[]{:S(2)}) collective-permute-start(bf16[8,24,3072]{2,1,0:T(8,128)(2,1)S(1)} %get-tuple-element.107), channel_id=1, source_target_pairs={{0,4},{1,5},{2,6},{3,7},{4,0},{5,1},{6,2},{7,3},{8,12},{9,13},{10,... | collective-permute-start | bytes 3538952 | tf_op jit(solution)/shard_map/ppermute | solution.py:552
  69.6 25.3 %copy-start.4 = (s32[2]{0:T(128)S(1)}, s32[2]{0:T(128)}, u32[]{:S(2)}) copy-start(s32[2]{0:T(128)} %copy-done.3) | copy-start | bytes 28
  97.8 18.3 %collective-permute-start.7 = (bf16[4,24,3072]{2,1,0:T(8,128)(2,1)S(1)}, bf16[4,24,3072]{2,1,0:T(8,128)(2,1)S(1)}, u32[]{:S(2)}, u32[]{:S(2)}) collective-permute-start(bf16[4,24,3072]{2,1,0:T(8,128)(2,1)S(1)} %get-tuple-element.113), channel_id=1, source_target_pairs={{0,4},{1,5},{2,6},{3,7},{4,0},{5,1},{6,2},{7,3},{8,12},{9,13},{10,... | collective-permute-start | bytes 1769480 | tf_op jit(solution)/shard_map/ppermute | solution.py:552
  99.5 19.9 %collective-permute-start.8 = (bf16[4,24,3072]{2,1,0:T(8,128)(2,1)S(1)}, bf16[4,24,3072]{2,1,0:T(8,128)(2,1)S(1)}, u32[]{:S(2)}, u32[]{:S(2)}) collective-permute-start(bf16[4,24,3072]{2,1,0:T(8,128)(2,1)S(1)} %get-tuple-element.114), channel_id=1, source_target_pairs={{0,2},{1,3},{2,0},{3,1},{4,6},{5,7},{6,4},{7,5},{8,10},{9,11},{10,... | collective-permute-start | bytes 1769480 | tf_op jit(solution)/shard_map/ppermute | solution.py:552
  106.3 13.1 %copy-start.5 = (s32[2]{0:T(128)S(1)}, s32[2]{0:T(128)}, u32[]{:S(2)}) copy-start(s32[2]{0:T(128)} %copy-done.3) | copy-start | bytes 28
  113.6 9.8 %collective-permute-start.9 = (bf16[4,4,256,128]{3,2,1,0:T(8,128)(2,1)}, bf16[4,4,256,128]{3,2,1,0:T(8,128)(2,1)S(1)}, u32[]{:S(2)}, u32[]{:S(2)}) collective-permute-start(bf16[4,4,256,128]{3,2,1,0:T(8,128)(2,1)} %get-tuple-element.123), channel_id=1, source_target_pairs={{0,1},{1,0},{2,3},{3,2},{4,5},{5,4},{6,7},{7,6},{8,9},{9,8},{10,11... | collective-permute-start | bytes 3145736 | tf_op jit(solution)/shard_map/ppermute | solution.py:829
  121.6 20.1 %collective-permute-start.10 = (bf16[2,24,6144]{2,1,0:T(8,128)(2,1)S(1)}, bf16[2,24,6144]{2,1,0:T(8,128)(2,1)S(1)}, u32[]{:S(2)}, u32[]{:S(2)}) collective-permute-start(bf16[2,24,6144]{2,1,0:T(8,128)(2,1)S(1)} %combine.10), channel_id=1, source_target_pairs={{0,8},{8,0},{16,24},{24,16},{1,9},{9,1},{17,25},{25,17},{2,10},{10... | collective-permute-start | bytes 1769480 | tf_op jit(solution)/shard_map/ppermute | solution.py:552
  124.1 17.6 %copy-start.8 = (bf16[4,256,128]{2,1,0:T(8,128)(2,1)}, bf16[4,256,128]{2,1,0:T(8,128)(2,1)S(1)}, u32[]{:S(2)}) copy-start(bf16[4,256,128]{2,1,0:T(8,128)(2,1)S(1)} %get-tuple-element.124.refs_15_) | copy-start | bytes 786436
  124.1 17.7 %collective-permute-start.11 = (bf16[4,256,128]{2,1,0:T(8,128)(2,1)S(1)}, bf16[4,256,128]{2,1,0:T(8,128)(2,1)S(1)}, u32[]{:S(2)}, u32[]{:S(2)}) collective-permute-start(bf16[4,256,128]{2,1,0:T(8,128)(2,1)S(1)} %get-tuple-element.132), channel_id=1, source_target_pairs={{0,2},{1,3},{2,0},{3,1},{4,6},{5,7},{6,4},{7,5},{8,10},{9,11},{10,... | collective-permute-start | bytes 786440 | tf_op jit(solution)/shard_map/ppermute | solution.py:845
  130.3 13.8 %collective-permute-start.12 = (bf16[4,256,128]{2,1,0:T(8,128)(2,1)S(1)}, bf16[4,256,128]{2,1,0:T(8,128)(2,1)S(1)}, u32[]{:S(2)}, u32[]{:S(2)}) collective-permute-start(bf16[4,256,128]{2,1,0:T(8,128)(2,1)S(1)} %get-tuple-element.133), channel_id=1, source_target_pairs={{0,4},{1,5},{2,6},{3,7},{4,0},{5,1},{6,2},{7,3},{8,12},{9,13},{10,... | collective-permute-start | bytes 786440 | tf_op jit(solution)/shard_map/ppermute | solution.py:845
  130.4 13.7 %collective-permute-start.13 = (bf16[4,256,128]{2,1,0:T(8,128)(2,1)S(1)}, bf16[4,256,128]{2,1,0:T(8,128)(2,1)S(1)}, u32[]{:S(2)}, u32[]{:S(2)}) collective-permute-start(bf16[4,256,128]{2,1,0:T(8,128)(2,1)S(1)} %get-tuple-element.134), channel_id=1, source_target_pairs={{0,6},{1,7},{2,4},{3,5},{4,2},{5,3},{6,0},{7,1},{8,14},{9,15},{10,... | collective-permute-start | bytes 786440 | tf_op jit(solution)/shard_map/ppermute | solution.py:845
  141.7 10.0 %collective-permute-start.14 = (bf16[32,24,768]{2,1,0:T(8,128)(2,1)}, bf16[32,24,768]{2,1,0:T(8,128)(2,1)S(1)}, u32[]{:S(2)}, u32[]{:S(2)}) collective-permute-start(bf16[32,24,768]{2,1,0:T(8,128)(2,1)} %bitcast.33), channel_id=1, source_target_pairs={{0,1},{1,0},{2,3},{3,2},{4,5},{5,4},{6,7},{7,6},{8,9},{9,8},{10,11... | collective-permute-start | bytes 3538952 | tf_op jit(solution)/shard_map/ppermute | solution.py:761
  146.1 24.7 %collective-permute-start.19 = (bf16[1,24,6144]{2,1,0:T(8,128)(2,1)S(1)}, bf16[1,24,6144]{2,1,0:T(8,128)(2,1)S(1)}, u32[]{:S(2)}, u32[]{:S(2)}) collective-permute-start(bf16[1,24,6144]{2,1,0:T(8,128)(2,1)S(1)} %combine.11), channel_id=1, source_target_pairs={{0,16},{8,24},{16,0},{24,8},{1,17},{9,25},{17,1},{25,9},{2,18},{10... | collective-permute-start | bytes 884744 | tf_op jit(solution)/shard_map/ppermute | solution.py:552
  152.4 12.0 %collective-permute-start.15 = (bf16[8,24,768]{2,1,0:T(8,128)(2,1)S(1)}, bf16[8,24,768]{2,1,0:T(8,128)(2,1)S(1)}, u32[]{:S(2)}, u32[]{:S(2)}) collective-permute-start(bf16[8,24,768]{2,1,0:T(8,128)(2,1)S(1)} %get-tuple-element.138), channel_id=1, source_target_pairs={{0,2},{1,3},{2,0},{3,1},{4,6},{5,7},{6,4},{7,5},{8,10},{9,11},{10,... | collective-permute-start | bytes 884744 | tf_op jit(solution)/shard_map/ppermute | solution.py:552
  153.0 11.4 %collective-permute-start.16 = (bf16[8,24,768]{2,1,0:T(8,128)(2,1)S(1)}, bf16[8,24,768]{2,1,0:T(8,128)(2,1)S(1)}, u32[]{:S(2)}, u32[]{:S(2)}) collective-permute-start(bf16[8,24,768]{2,1,0:T(8,128)(2,1)S(1)} %get-tuple-element.139), channel_id=1, source_target_pairs={{0,4},{1,5},{2,6},{3,7},{4,0},{5,1},{6,2},{7,3},{8,12},{9,13},{10,... | collective-permute-start | bytes 884744 | tf_op jit(solution)/shard_map/ppermute | solution.py:552
  164.3 1.7 collective-permute-start.18
  166.6 9.1 %collective-permute-start.21 = (bf16[4,24,256]{2,1,0:T(8,128)(2,1)S(1)}, bf16[4,24,256]{2,1,0:T(8,128)(2,1)S(1)}, u32[]{:S(2)}, u32[]{:S(2)}) collective-permute-start(bf16[4,24,256]{2,1,0:T(8,128)(2,1)S(1)} %get-tuple-element.149), channel_id=1, source_target_pairs={{0,2},{1,3},{2,0},{3,1},{4,6},{5,7},{6,4},{7,5},{8,10},{9,11},{10,... | collective-permute-start | bytes 147464 | tf_op jit(solution)/shard_map/ppermute | solution.py:581
  167.1 8.6 %collective-permute-start.17 = (bf16[4,24,768]{2,1,0:T(8,128)(2,1)S(1)}, bf16[4,24,768]{2,1,0:T(8,128)(2,1)S(1)}, u32[]{:S(2)}, u32[]{:S(2)}) collective-permute-start(bf16[4,24,768]{2,1,0:T(8,128)(2,1)S(1)} %get-tuple-element.145), channel_id=1, source_target_pairs={{0,4},{1,5},{2,6},{3,7},{4,0},{5,1},{6,2},{7,3},{8,12},{9,13},{10,... | collective-permute-start | bytes 442376 | tf_op jit(solution)/shard_map/ppermute | solution.py:552
  168.4 7.3 %collective-permute-start.20 = (bf16[4,24,768]{2,1,0:T(8,128)(2,1)S(1)}, bf16[4,24,768]{2,1,0:T(8,128)(2,1)S(1)}, u32[]{:S(2)}, u32[]{:S(2)}) collective-permute-start(bf16[4,24,768]{2,1,0:T(8,128)(2,1)S(1)} %get-tuple-element.146), channel_id=1, source_target_pairs={{0,2},{1,3},{2,0},{3,1},{4,6},{5,7},{6,4},{7,5},{8,10},{9,11},{10,... | collective-permute-start | bytes 442376 | tf_op jit(solution)/shard_map/ppermute | solution.py:552
  169.0 5.7 %collective-permute-start.22 = (bf16[4,24,256]{2,1,0:T(8,128)(2,1)S(1)}, bf16[4,24,256]{2,1,0:T(8,128)(2,1)S(1)}, u32[]{:S(2)}, u32[]{:S(2)}) collective-permute-start(bf16[4,24,256]{2,1,0:T(8,128)(2,1)S(1)} %get-tuple-element.153), channel_id=1, source_target_pairs={{0,4},{1,5},{2,6},{3,7},{4,0},{5,1},{6,2},{7,3},{8,12},{9,13},{10,... | collective-permute-start | bytes 147464 | tf_op jit(solution)/shard_map/ppermute | solution.py:581
  170.8 5.0 %collective-permute-start.23 = (bf16[4,24,256]{2,1,0:T(8,128)(2,1)S(1)}, bf16[4,24,256]{2,1,0:T(8,128)(2,1)S(1)}, u32[]{:S(2)}, u32[]{:S(2)}) collective-permute-start(bf16[4,24,256]{2,1,0:T(8,128)(2,1)S(1)} %get-tuple-element.154), channel_id=1, source_target_pairs={{0,6},{1,7},{2,4},{3,5},{4,2},{5,3},{6,0},{7,1},{8,14},{9,15},{10,... | collective-permute-start | bytes 147464 | tf_op jit(solution)/shard_map/ppermute | solution.py:581
  176.5 5.1 %collective-permute-start.24 = (bf16[1,24,1792]{2,1,0:T(8,128)(2,1)S(1)}, bf16[1,24,1792]{2,1,0:T(8,128)(2,1)S(1)}, u32[]{:S(2)}, u32[]{:S(2)}) collective-permute-start(bf16[1,24,1792]{2,1,0:T(8,128)(2,1)S(1)} %get-tuple-element.155), channel_id=1, source_target_pairs={{0,8},{8,0},{16,24},{24,16},{1,9},{9,1},{17,25},{25,17},{2,10},{10... | collective-permute-start | bytes 258056 | tf_op jit(solution)/shard_map/ppermute | solution.py:581
  177.9 8.1 %collective-permute-start.25 = (bf16[1,24,1792]{2,1,0:T(8,128)(2,1)S(1)}, bf16[1,24,1792]{2,1,0:T(8,128)(2,1)S(1)}, u32[]{:S(2)}, u32[]{:S(2)}) collective-permute-start(bf16[1,24,1792]{2,1,0:T(8,128)(2,1)S(1)} %get-tuple-element.156), channel_id=1, source_target_pairs={{0,16},{8,24},{16,0},{24,8},{1,17},{9,25},{17,1},{25,9},{2,18},{10... | collective-permute-start | bytes 258056 | tf_op jit(solution)/shard_map/ppermute | solution.py:581
  177.9 8.0 %collective-permute-start.26 = (bf16[1,24,1792]{2,1,0:T(8,128)(2,1)S(1)}, bf16[1,24,1792]{2,1,0:T(8,128)(2,1)S(1)}, u32[]{:S(2)}, u32[]{:S(2)}) collective-permute-start(bf16[1,24,1792]{2,1,0:T(8,128)(2,1)S(1)} %get-tuple-element.157), channel_id=1, source_target_pairs={{0,24},{8,16},{16,8},{24,0},{1,25},{9,17},{17,9},{25,1},{2,26},{10... | collective-permute-start | bytes 258056 | tf_op jit(solution)/shard_map/ppermute | solution.py:581
  (10 other events, 43.9 us)

commit v2 on v1

--- a/solution.py
+++ b/solution.py
@@ -143,7 +143,8 @@
         din_ref[...] = jnp.zeros_like(din_ref)
 
     bupg_ref[...] = jnp.zeros_like(bupg_ref)
-    bias = bup_ref[...].astype(F32)
+    bias = bup_ref[pl.ds(pl.multiple_of(pl.program_id(0) * up_ref.shape[1], LANES), up_ref.shape[1])]
+    bias = bias.astype(F32).reshape(1, up_ref.shape[1])
 
     def step(i, carry):
         at = pl.ds(pl.multiple_of(i * chunk, chunk), chunk)
@@ -712,7 +713,7 @@
                 whole((token_count, width)), whole((token_count, width)),
                 whole((width, token_count)), whole((width, token_count)),
                 pl.BlockSpec((width, tile), lambda f, *_: (0, f)),
-                pl.BlockSpec((1, tile), lambda f, *_: (0, f)),
+                whole((hidden,)),
                 pl.BlockSpec((tile, width), lambda f, *_: (f, 0)),
             ],
             out_specs=[
@@ -732,7 +733,7 @@
         compiler_params=params(60),
         cost_estimate=LONG,
         name="mlp",
-    )(side, mlp_in, bg, joined(mlp_t), joined(bg_t), w_up, b_up.reshape(1, hidden), w_down)
+    )(side, mlp_in, bg, joined(mlp_t), joined(bg_t), w_up, b_up, w_down)
 
     gathered = ordered_after(tuple(gathered), b_up_part)
 

time: 188 us -> 189 us (level)
  starting transfers between devices: 47 us -> 50.6 us
    ppermute x10, starting transfers between devices: 23.4 us -> 29.4 us  [reduce_level(): lax.ppermute(send, AXES[axis], partners(lax.axis_size(AXES[axis]), 1 << b...]
    ppermute x3, starting transfers between devices: 7.72 us -> 5.51 us  [on_device(): lax.ppermute(shares[j], 'seq', partners(seq_devices, 2 * j))]
  transfers between devices with their start and end apart: 27 -> 27, of which waited for: 9 -> 10; matrix products, arithmetic and copies ran while one was open for 2% -> 1% of each run, Pallas kernels for 50% -> 49%
where the time goes in v2:
time: 189 us; the launch traced here: 190 us
  Pallas kernels  107 us (57%)
  starting transfers between devices  50.6 us (27%)
  waiting for transfers between devices  26.6 us (14%)
  local copies, waits for them, and re-layouts  2.4 us (1%)
  other arithmetic  2.19 us (1%)
    pallas_call x1, Pallas kernels, on_device(): pl.pallas_call(functools.partial(mlp_kernel, token_count), grid_spec=pltp...  37.8 us
    ppermute x10, starting transfers between devices, reduce_level(): lax.ppermute(send, AXES[axis], partners(lax.axis_size(AXES[axis]), 1 << b...  29.4 us
    pallas_call x2, Pallas kernels, attention(): pl.pallas_call(functools.partial(attention_kernel, heads, head_size, seq_...  22.7 us
    pallas_call x11, Pallas kernels, call_on_terms(): pl.pallas_call(body, grid_spec=pltpu.PrefetchScalarGridSpec(num_scalar_pr...  17.9 us
    ppermute x10, waiting for transfers between devices, reduce_level(): lax.ppermute(send, AXES[axis], partners(lax.axis_size(AXES[axis]), 1 << b...  13.1 us
    pallas_call x1, Pallas kernels, on_device(): pl.pallas_call(mix_kernel, grid_spec=pltpu.PrefetchScalarGridSpec(num_sca...  9.87 us
    pallas_call x1, Pallas kernels, on_device(): pl.pallas_call(exit_body, grid_spec=pltpu.PrefetchScalarGridSpec(num_scal...  9.68 us
    pallas_call x1, Pallas kernels, on_device(): pl.pallas_call(functools.partial(entry_kernel, head_size, order_a, order_...  9.05 us
  transfers between devices with their start and end apart: 27, of which 10 were waited for; matrix products, arithmetic and copies ran while one was open for 1% of the time, Pallas kernels for 49%

profile of v2, /device:TPU:0, one launch (start us, length us, event | category | flops | bytes accessed | tf_op | source)
XLA Modules:
  0.0 189.9 jit_solution(3198711747135864320)
XLA Ops:
  1.4 9.1 %entry.1 = (bf16[1024,768]{1,0:T(8,128)(2,1)}, bf16[1024,768]{1,0:T(8,128)(2,1)}, bf16[768,1024]{1,0:T(8,128)(2,1)}, bf16[768,1024]{1,0:T(8,128)(2,1)}, bf16[768...) custom-call(bf16[4,256,768]{2,1,0:T(8,128)(2,1)} %refs_1_.1, ...), custom_call_target="tpu_custom_call" | custom-call | flops 40000000000 | bytes 10000000 | tf_op jit(solution)/shard_map/entry/pallas_call | solution.py:664
  10.5 4.0 %collective-permute-start.2 = (bf16[4,272,128]{2,1,0:T(8,128)(2,1)}, bf16[4,272,128]{2,1,0:T(8,128)(2,1)S(1)}, u32[]{:S(2)}, u32[]{:S(2)}) collective-permute-start(bf16[4,272,128]{2,1,0:T(8,128)(2,1)} %get-tuple-element.99.refs_0_), channel_id=1, source_target_pairs={{0,6},{1,7},{2,4},{3,5},{4,2},{5,3},{6,0},{7,1},{8,14},{9,15},{10,... | collective-permute-start | bytes 835592 | tf_op jit(solution)/shard_map/ppermute | solution.py:701
  15.1 37.8 %mlp.1 = (bf16[2,384,3072]{2,1,0:T(8,128)(2,1)}, bf16[2,384,3072]{2,1,0:T(8,128)(2,1)}, f32[1024,768]{1,0:T(8,128)}, f32[1024,768]{1,0:T(8,128)}, f32[1,3072]{1,0:T(1,128)}) custom-call(s32[1]{0:T(128)} %bitcast.side_ref.refs_0_, bf16[1024,768]{1,0:T(8,128)(2,1)} %get-tuple-element.94.mlp_ref, bf16[1024,768]{1,0:T(8,128)(2,1)} %get-tuple-element.95.bg_ref, ...), custom_call_target="tpu_custom_call" | custom-call | flops 40000000000 | bytes 10000000 | tf_op jit(solution)/shard_map/mlp/pallas_call | solution.py:707
  53.5 1.4 reduce.3
  56.4 4.7 %collective-permute-done.3.refs_1_.refs_3_.refs_4_.refs_5_.refs_6_.refs_7_ = bf16[32,24,3072]{2,1,0:T(8,128)(2,1)} collective-permute-done((bf16[32,24,3072]{2,1,0:T(8,128)(2,1)}, bf16[32,24,3072]{2,1,0:T(8,128)(2,1)}, u32[]{:S(2)}, u32[]{:S(2)}) %collective-permute-start.3) | collective-permute-done | bytes 4718624 | tf_op jit(solution)/shard_map/ppermute | solution.py:762
  61.2 3.2 %combine.8 = (bf16[8,24,3072]{2,1,0:T(8,128)(2,1)S(1)}, bf16[8,24,3072]{2,1,0:T(8,128)(2,1)S(1)}) custom-call(s32[2]{0:T(128)S(1)} %pad_add_fusion.where_ref, bf16[32,24,3072]{2,1,0:T(8,128)(2,1)} %bitcast.36, bf16[32,24,3072]{2,1,0:T(8,128)(2,1)} %collective-permute-done.3.refs_1_.refs_3_.refs_4_.refs_5_.refs_6_.refs_7_, bf16[32,24,3072]{2,1,0:T(8,128)(2,1)} %bitcast.37, ...), custom_call_target="tpu_custom_call" | custom-call | flops 40000000000 | bytes 10000000 | tf_op jit(solution)/shard_map/combine/pallas_call | solution.py:463
  64.4 2.0 %collective-permute-start.5 = (bf16[8,24,3072]{2,1,0:T(8,128)(2,1)S(1)}, bf16[8,24,3072]{2,1,0:T(8,128)(2,1)S(1)}, u32[]{:S(2)}, u32[]{:S(2)}) collective-permute-start(bf16[8,24,3072]{2,1,0:T(8,128)(2,1)S(1)} %get-tuple-element.106), channel_id=1, source_target_pairs={{0,2},{1,3},{2,0},{3,1},{4,6},{5,7},{6,4},{7,5},{8,10},{9,11},{10,... | collective-permute-start | bytes 3538952 | tf_op jit(solution)/shard_map/ppermute | solution.py:553
  66.4 1.5 collective-permute-start.6
  68.9 15.4 %attention.2 = (bf16[768,1024]{1,0:T(8,128)(2,1)}, bf16[768,1024]{1,0:T(8,128)(2,1)}, bf16[4,4,256,128]{3,2,1,0:T(8,128)(2,1)}, bf16[4,4,256,128]{3,2,1,0:T(8,128)(2,1)}) custom-call(s32[2]{0:T(128)} %copy-done.3, s32[4,256]{1,0:T(4,128)} %refs_3_.1, bf16[4,64,3072]{2,1,0:T(8,128)(2,1)} %get-tuple-element.109.q_t_ref, ...), custom_call_target="tpu_custom_call" | custom-call | flops 40000000000 | bytes 10000000 | tf_op jit(solution)/shard_map/attention/pallas_call | solution.py:782
  84.3 8.4 %collective-permute-done.5.refs_2_ = bf16[8,24,3072]{2,1,0:T(8,128)(2,1)S(1)} collective-permute-done((bf16[8,24,3072]{2,1,0:T(8,128)(2,1)S(1)}, bf16[8,24,3072]{2,1,0:T(8,128)(2,1)S(1)}, u32[]{:S(2)}, u32[]{:S(2)}) %collective-permute-start.5) | collective-permute-done | bytes 1179680 | tf_op jit(solution)/shard_map/ppermute | solution.py:553
  92.6 1.6 collective-permute-done.6.refs_5_.refs_6_.refs_7_.refs_8_
  94.2 2.9 %combine.9 = (bf16[4,24,3072]{2,1,0:T(8,128)(2,1)S(1)}, bf16[4,24,3072]{2,1,0:T(8,128)(2,1)S(1)}) custom-call(s32[2]{0:T(128)S(1)} %copy-done.4, bf16[32,24,3072]{2,1,0:T(8,128)(2,1)} %bitcast.38, bf16[32,24,3072]{2,1,0:T(8,128)(2,1)} %collective-permute-done.3.refs_1_.refs_3_.refs_4_.refs_5_.refs_6_.refs_7_, bf16[8,24,3072]{2,1,0:T(8,128)(2,1)} %copy-done.9, ...), custom_call_target="tpu_custom_call" | custom-call | flops 40000000000 | bytes 10000000 | tf_op jit(solution)/shard_map/combine/pallas_call | solution.py:463
  97.1 11.7 %collective-permute-start.7 = (bf16[4,24,3072]{2,1,0:T(8,128)(2,1)S(1)}, bf16[4,24,3072]{2,1,0:T(8,128)(2,1)S(1)}, u32[]{:S(2)}, u32[]{:S(2)}) collective-permute-start(bf16[4,24,3072]{2,1,0:T(8,128)(2,1)S(1)} %get-tuple-element.113), channel_id=1, source_target_pairs={{0,4},{1,5},{2,6},{3,7},{4,0},{5,1},{6,2},{7,3},{8,12},{9,13},{10,... | collective-permute-start | bytes 1769480 | tf_op jit(solution)/shard_map/ppermute | solution.py:553
  108.8 7.3 %attention.3 = (bf16[768,1024]{1,0:T(8,128)(2,1)}, bf16[768,1024]{1,0:T(8,128)(2,1)}, bf16[4,4,256,128]{3,2,1,0:T(8,128)(2,1)}, bf16[4,4,256,128]{3,2,1,0:T(8,128)(2,1)}) custom-call(s32[2]{0:T(128)} %copy-done.3, s32[4,256]{1,0:T(4,128)} %refs_3_.1, ...), custom_call_target="tpu_custom_call", output_to_operand_aliasing={{0}: (8, {}), {1}: (9, {}), {2}: (10, {}), {3}: (11, {})} | custom-call | flops 40000000000 | bytes 10000000 | tf_op jit(solution)/shard_map/attention/pallas_call | solution.py:782
  116.2 2.7 %collective-permute-start.9 = (bf16[4,4,256,128]{3,2,1,0:T(8,128)(2,1)}, bf16[4,4,256,128]{3,2,1,0:T(8,128)(2,1)S(1)}, u32[]{:S(2)}, u32[]{:S(2)}) collective-permute-start(bf16[4,4,256,128]{3,2,1,0:T(8,128)(2,1)} %get-tuple-element.123), channel_id=1, source_target_pairs={{0,1},{1,0},{2,3},{3,2},{4,5},{5,4},{6,7},{7,6},{8,9},{9,8},{10,11... | collective-permute-start | bytes 3145736 | tf_op jit(solution)/shard_map/ppermute | solution.py:830
  118.9 3.1 %collective-permute-done.8.refs_7_.refs_8_.refs_9_ = bf16[4,24,3072]{2,1,0:T(8,128)(2,1)S(1)} collective-permute-done((bf16[4,24,3072]{2,1,0:T(8,128)(2,1)S(1)}, bf16[4,24,3072]{2,1,0:T(8,128)(2,1)S(1)}, u32[]{:S(2)}, u32[]{:S(2)}) %collective-permute-start.8) | collective-permute-done | bytes 589856 | tf_op jit(solution)/shard_map/ppermute | solution.py:553
  122.0 2.3 %combine.10 = bf16[2,24,6144]{2,1,0:T(8,128)(2,1)S(1)} custom-call(s32[2]{0:T(128)S(1)} %copy-done.5, bf16[32,24,3072]{2,1,0:T(8,128)(2,1)} %bitcast.40, bf16[32,24,3072]{2,1,0:T(8,128)(2,1)} %collective-permute-done.3.refs_1_.refs_3_.refs_4_.refs_5_.refs_6_.refs_7_, bf16[8,24,3072]{2,1,0:T(8,128)(2,1)} %copy-done.9, ...), custom_call_target="tpu_custom_call" | custom-call | flops 40000000000 | bytes 10000000 | tf_op jit(solution)/shard_map/combine/pallas_call | solution.py:463
  124.3 9.6 %collective-permute-start.10 = (bf16[2,24,6144]{2,1,0:T(8,128)(2,1)S(1)}, bf16[2,24,6144]{2,1,0:T(8,128)(2,1)S(1)}, u32[]{:S(2)}, u32[]{:S(2)}) collective-permute-start(bf16[2,24,6144]{2,1,0:T(8,128)(2,1)S(1)} %combine.10), channel_id=1, source_target_pairs={{0,8},{8,0},{16,24},{24,16},{1,9},{9,1},{17,25},{25,17},{2,10},{10... | collective-permute-start | bytes 1769480 | tf_op jit(solution)/shard_map/ppermute | solution.py:553
  134.7 4.0 %collective-permute-start.11 = (bf16[4,256,128]{2,1,0:T(8,128)(2,1)S(1)}, bf16[4,256,128]{2,1,0:T(8,128)(2,1)S(1)}, u32[]{:S(2)}, u32[]{:S(2)}) collective-permute-start(bf16[4,256,128]{2,1,0:T(8,128)(2,1)S(1)} %get-tuple-element.132), channel_id=1, source_target_pairs={{0,2},{1,3},{2,0},{3,1},{4,6},{5,7},{6,4},{7,5},{8,10},{9,11},{10,... | collective-permute-start | bytes 786440 | tf_op jit(solution)/shard_map/ppermute | solution.py:846
  138.7 1.5 collective-permute-start.13
  140.2 9.9 %mix.1 = (bf16[4,256,768]{2,1,0:T(8,128)(2,1)}, bf16[2,384,768]{2,1,0:T(8,128)(2,1)}, bf16[2,384,768]{2,1,0:T(8,128)(2,1)}) custom-call(s32[1]{0:T(128)} %bitcast.side_ref.refs_0_, bf16[4,256,768]{2,1,0:T(8,128)(2,1)} %refs_1_.1, s32[4,256]{1,0:T(4,128)} %refs_3_.1, bf16[768,1024]{1,0:T(8,128)(2,1)} %get-tuple-element.119.mix_t_ref, ...), custom_call_target="tpu_custom_call" | custom-call | flops 40000000000 | bytes 10000000 | tf_op jit(solution)/shard_map/mix/pallas_call | solution.py:850
  150.2 1.8 collective-permute-done.12.refs_17_
  152.0 2.0 %combine.11 = bf16[1,24,6144]{2,1,0:T(8,128)(2,1)S(1)} custom-call(s32[2]{0:T(128)S(1)} %copy-done.5, bf16[32,24,3072]{2,1,0:T(8,128)(2,1)} %bitcast.42, bf16[32,24,3072]{2,1,0:T(8,128)(2,1)} %collective-permute-done.3.refs_1_.refs_3_.refs_4_.refs_5_.refs_6_.refs_7_, bf16[8,24,3072]{2,1,0:T(8,128)(2,1)} %copy-done.9, ...), custom_call_target="tpu_custom_call" | custom-call | flops 40000000000 | bytes 10000000 | tf_op jit(solution)/shard_map/combine/pallas_call | solution.py:463
  154.8 1.1 collective-permute-start.15
  156.6 9.7 %exit.1 = (bf16[4,256,768]{2,1,0:T(8,128)(2,1)}, bf16[384,256]{1,0:T(8,128)(2,1)}, bf16[384,256]{1,0:T(8,128)(2,1)}) custom-call(s32[1]{0:T(128)} %bitcast.side_ref.refs_0_, bf16[4,256,768]{2,1,0:T(8,128)(2,1)} %refs_1_.1, bf16[4,256,768]{2,1,0:T(8,128)(2,1)} %refs_2_.1, s32[4,256]{1,0:T(4,128)} %refs_3_.1, ...), custom_call_target="tpu_custom_call" | custom-call | flops 40000000000 | bytes 10000000 | tf_op jit(solution)/shard_map/exit/pallas_call | solution.py:894
  169.2 1.7 collective-permute-start.17
  172.7 1.8 collective-permute-start.23
  174.5 2.7 %own.2 = (f32[24,3072]{1,0:T(8,128)}, f32[24,3072]{1,0:T(8,128)}) custom-call(s32[2]{0:T(128)S(1)} %copy-done.5, bf16[32,24,3072]{2,1,0:T(8,128)(2,1)} %bitcast.44, bf16[32,24,3072]{2,1,0:T(8,128)(2,1)} %collective-permute-done.3.refs_1_.refs_3_.refs_4_.refs_5_.refs_6_.refs_7_, bf16[8,24,3072]{2,1,0:T(8,128)(2,1)} %copy-done.9, ...), custom_call_target="tpu_custom_call" | custom-call | flops 40000000000 | bytes 10000000 | tf_op jit(solution)/shard_map/own/pallas_call | solution.py:463
  179.3 2.9 %collective-permute-start.25 = (bf16[1,24,1792]{2,1,0:T(8,128)(2,1)S(1)}, bf16[1,24,1792]{2,1,0:T(8,128)(2,1)S(1)}, u32[]{:S(2)}, u32[]{:S(2)}) collective-permute-start(bf16[1,24,1792]{2,1,0:T(8,128)(2,1)S(1)} %get-tuple-element.156), channel_id=1, source_target_pairs={{0,16},{8,24},{16,0},{24,8},{1,17},{9,25},{17,1},{25,9},{2,18},{10... | collective-permute-start | bytes 258056 | tf_op jit(solution)/shard_map/ppermute | solution.py:582
  183.0 4.4 %collective-permute-done.25.refs_5_.refs_12_.refs_20_ = bf16[1,24,1792]{2,1,0:T(8,128)(2,1)S(1)} collective-permute-done((bf16[1,24,1792]{2,1,0:T(8,128)(2,1)S(1)}, bf16[1,24,1792]{2,1,0:T(8,128)(2,1)S(1)}, u32[]{:S(2)}, u32[]{:S(2)}) %collective-permute-start.25) | collective-permute-done | bytes 86048 | tf_op jit(solution)/shard_map/ppermute | solution.py:582
  187.4 1.1 collective-permute-done.26.refs_6_.refs_13_.refs_21_
  188.5 1.3 own.3
  (77 shorter events, 14.4 us)
Async XLA Ops:
  10.5 45.3 %collective-permute-start.2 = (bf16[4,272,128]{2,1,0:T(8,128)(2,1)}, bf16[4,272,128]{2,1,0:T(8,128)(2,1)S(1)}, u32[]{:S(2)}, u32[]{:S(2)}) collective-permute-start(bf16[4,272,128]{2,1,0:T(8,128)(2,1)} %get-tuple-element.99.refs_0_), channel_id=1, source_target_pairs={{0,6},{1,7},{2,4},{3,5},{4,2},{5,3},{6,0},{7,1},{8,14},{9,15},{10,... | collective-permute-start | bytes 835592 | tf_op jit(solution)/shard_map/ppermute | solution.py:701
  14.4 41.4 %collective-permute-start.1 = (bf16[4,272,128]{2,1,0:T(8,128)(2,1)}, bf16[4,272,128]{2,1,0:T(8,128)(2,1)S(1)}, u32[]{:S(2)}, u32[]{:S(2)}) collective-permute-start(bf16[4,272,128]{2,1,0:T(8,128)(2,1)} %get-tuple-element.99.refs_0_), channel_id=1, source_target_pairs={{0,4},{1,5},{2,6},{3,7},{4,0},{5,1},{6,2},{7,3},{8,12},{9,13},{10,... | collective-permute-start | bytes 835592 | tf_op jit(solution)/shard_map/ppermute | solution.py:701
  14.9 40.8 %collective-permute-start = (bf16[4,272,128]{2,1,0:T(8,128)(2,1)}, bf16[4,272,128]{2,1,0:T(8,128)(2,1)S(1)}, u32[]{:S(2)}, u32[]{:S(2)}) collective-permute-start(bf16[4,272,128]{2,1,0:T(8,128)(2,1)} %get-tuple-element.99.refs_0_), channel_id=1, source_target_pairs={{0,2},{1,3},{2,0},{3,1},{4,6},{5,7},{6,4},{7,5},{8,10},{9,11},{10,... | collective-permute-start | bytes 835592 | tf_op jit(solution)/shard_map/ppermute | solution.py:701
  15.1 40.7 %copy-start.7 = (bf16[4,272,128]{2,1,0:T(8,128)(2,1)S(1)}, bf16[4,272,128]{2,1,0:T(8,128)(2,1)}, u32[]{:S(2)}) copy-start(bf16[4,272,128]{2,1,0:T(8,128)(2,1)} %get-tuple-element.99.refs_0_) | copy-start | bytes 835588
  52.9 8.3 %collective-permute-start.3 = (bf16[32,24,3072]{2,1,0:T(8,128)(2,1)}, bf16[32,24,3072]{2,1,0:T(8,128)(2,1)}, u32[]{:S(2)}, u32[]{:S(2)}) collective-permute-start(bf16[32,24,3072]{2,1,0:T(8,128)(2,1)} %bitcast.32), channel_id=1, source_target_pairs={{0,1},{1,0},{2,3},{3,2},{4,5},{5,4},{6,7},{7,6},{8,9},{9,8},{10,11... | collective-permute-start | bytes 14155784 | tf_op jit(solution)/shard_map/ppermute | solution.py:762
  55.9 12.0 %collective-permute-start.4 = (bf16[4,4,272,128]{3,2,1,0:T(8,128)(2,1)S(1)}, bf16[4,4,272,128]{3,2,1,0:T(8,128)(2,1)S(1)}, u32[]{:S(2)}, u32[]{:S(2)}) collective-permute-start(bf16[4,4,272,128]{3,2,1,0:T(8,128)(2,1)S(1)} %stack.13.even_ref), channel_id=1, source_target_pairs={{0,1},{1,0},{2,3},{3,2},{4,5},{5,4},{6,7},{7,6},{8,9},{9,8},{10,11... | collective-permute-start | bytes 3342344 | tf_op jit(solution)/shard_map/ppermute | solution.py:753
  64.4 28.2 %collective-permute-start.5 = (bf16[8,24,3072]{2,1,0:T(8,128)(2,1)S(1)}, bf16[8,24,3072]{2,1,0:T(8,128)(2,1)S(1)}, u32[]{:S(2)}, u32[]{:S(2)}) collective-permute-start(bf16[8,24,3072]{2,1,0:T(8,128)(2,1)S(1)} %get-tuple-element.106), channel_id=1, source_target_pairs={{0,2},{1,3},{2,0},{3,1},{4,6},{5,7},{6,4},{7,5},{8,10},{9,11},{10,... | collective-permute-start | bytes 3538952 | tf_op jit(solution)/shard_map/ppermute | solution.py:553
  66.4 27.8 %collective-permute-start.6 = (bf16[8,24,3072]{2,1,0:T(8,128)(2,1)S(1)}, bf16[8,24,3072]{2,1,0:T(8,128)(2,1)}, u32[]{:S(2)}, u32[]{:S(2)}) collective-permute-start(bf16[8,24,3072]{2,1,0:T(8,128)(2,1)S(1)} %get-tuple-element.107), channel_id=1, source_target_pairs={{0,4},{1,5},{2,6},{3,7},{4,0},{5,1},{6,2},{7,3},{8,12},{9,13},{10,... | collective-permute-start | bytes 3538952 | tf_op jit(solution)/shard_map/ppermute | solution.py:553
  68.9 25.3 %copy-start.4 = (s32[2]{0:T(128)S(1)}, s32[2]{0:T(128)}, u32[]{:S(2)}) copy-start(s32[2]{0:T(128)} %copy-done.3) | copy-start | bytes 28
  97.1 21.8 %collective-permute-start.7 = (bf16[4,24,3072]{2,1,0:T(8,128)(2,1)S(1)}, bf16[4,24,3072]{2,1,0:T(8,128)(2,1)S(1)}, u32[]{:S(2)}, u32[]{:S(2)}) collective-permute-start(bf16[4,24,3072]{2,1,0:T(8,128)(2,1)S(1)} %get-tuple-element.113), channel_id=1, source_target_pairs={{0,4},{1,5},{2,6},{3,7},{4,0},{5,1},{6,2},{7,3},{8,12},{9,13},{10,... | collective-permute-start | bytes 1769480 | tf_op jit(solution)/shard_map/ppermute | solution.py:553
  108.8 13.2 %collective-permute-start.8 = (bf16[4,24,3072]{2,1,0:T(8,128)(2,1)S(1)}, bf16[4,24,3072]{2,1,0:T(8,128)(2,1)S(1)}, u32[]{:S(2)}, u32[]{:S(2)}) collective-permute-start(bf16[4,24,3072]{2,1,0:T(8,128)(2,1)S(1)} %get-tuple-element.114), channel_id=1, source_target_pairs={{0,2},{1,3},{2,0},{3,1},{4,6},{5,7},{6,4},{7,5},{8,10},{9,11},{10,... | collective-permute-start | bytes 1769480 | tf_op jit(solution)/shard_map/ppermute | solution.py:553
  108.8 13.2 %copy-start.5 = (s32[2]{0:T(128)S(1)}, s32[2]{0:T(128)}, u32[]{:S(2)}) copy-start(s32[2]{0:T(128)} %copy-done.3) | copy-start | bytes 28
  116.2 17.7 %copy-start.2 = (bf16[4,4,256,128]{3,2,1,0:T(8,128)(2,1)S(1)}, bf16[4,4,256,128]{3,2,1,0:T(8,128)(2,1)}, u32[]{:S(2)}) copy-start(bf16[4,4,256,128]{3,2,1,0:T(8,128)(2,1)} %get-tuple-element.122.keep_ref) | copy-start | bytes 3145732
  116.2 17.7 %collective-permute-start.9 = (bf16[4,4,256,128]{3,2,1,0:T(8,128)(2,1)}, bf16[4,4,256,128]{3,2,1,0:T(8,128)(2,1)S(1)}, u32[]{:S(2)}, u32[]{:S(2)}) collective-permute-start(bf16[4,4,256,128]{3,2,1,0:T(8,128)(2,1)} %get-tuple-element.123), channel_id=1, source_target_pairs={{0,1},{1,0},{2,3},{3,2},{4,5},{5,4},{6,7},{7,6},{8,9},{9,8},{10,11... | collective-permute-start | bytes 3145736 | tf_op jit(solution)/shard_map/ppermute | solution.py:830
  124.3 25.9 %collective-permute-start.10 = (bf16[2,24,6144]{2,1,0:T(8,128)(2,1)S(1)}, bf16[2,24,6144]{2,1,0:T(8,128)(2,1)S(1)}, u32[]{:S(2)}, u32[]{:S(2)}) collective-permute-start(bf16[2,24,6144]{2,1,0:T(8,128)(2,1)S(1)} %combine.10), channel_id=1, source_target_pairs={{0,8},{8,0},{16,24},{24,16},{1,9},{9,1},{17,25},{25,17},{2,10},{10... | collective-permute-start | bytes 1769480 | tf_op jit(solution)/shard_map/ppermute | solution.py:553
  134.7 15.4 %copy-start.8 = (bf16[4,256,128]{2,1,0:T(8,128)(2,1)}, bf16[4,256,128]{2,1,0:T(8,128)(2,1)S(1)}, u32[]{:S(2)}) copy-start(bf16[4,256,128]{2,1,0:T(8,128)(2,1)S(1)} %get-tuple-element.124.refs_15_) | copy-start | bytes 786436
  134.7 15.5 %collective-permute-start.11 = (bf16[4,256,128]{2,1,0:T(8,128)(2,1)S(1)}, bf16[4,256,128]{2,1,0:T(8,128)(2,1)S(1)}, u32[]{:S(2)}, u32[]{:S(2)}) collective-permute-start(bf16[4,256,128]{2,1,0:T(8,128)(2,1)S(1)} %get-tuple-element.132), channel_id=1, source_target_pairs={{0,2},{1,3},{2,0},{3,1},{4,6},{5,7},{6,4},{7,5},{8,10},{9,11},{10,... | collective-permute-start | bytes 786440 | tf_op jit(solution)/shard_map/ppermute | solution.py:846
  138.7 13.3 %collective-permute-start.12 = (bf16[4,256,128]{2,1,0:T(8,128)(2,1)S(1)}, bf16[4,256,128]{2,1,0:T(8,128)(2,1)S(1)}, u32[]{:S(2)}, u32[]{:S(2)}) collective-permute-start(bf16[4,256,128]{2,1,0:T(8,128)(2,1)S(1)} %get-tuple-element.133), channel_id=1, source_target_pairs={{0,4},{1,5},{2,6},{3,7},{4,0},{5,1},{6,2},{7,3},{8,12},{9,13},{10,... | collective-permute-start | bytes 786440 | tf_op jit(solution)/shard_map/ppermute | solution.py:846
  138.7 13.3 %collective-permute-start.13 = (bf16[4,256,128]{2,1,0:T(8,128)(2,1)S(1)}, bf16[4,256,128]{2,1,0:T(8,128)(2,1)S(1)}, u32[]{:S(2)}, u32[]{:S(2)}) collective-permute-start(bf16[4,256,128]{2,1,0:T(8,128)(2,1)S(1)} %get-tuple-element.134), channel_id=1, source_target_pairs={{0,6},{1,7},{2,4},{3,5},{4,2},{5,3},{6,0},{7,1},{8,14},{9,15},{10,... | collective-permute-start | bytes 786440 | tf_op jit(solution)/shard_map/ppermute | solution.py:846
  150.1 4.0 %collective-permute-start.14 = (bf16[32,24,768]{2,1,0:T(8,128)(2,1)}, bf16[32,24,768]{2,1,0:T(8,128)(2,1)S(1)}, u32[]{:S(2)}, u32[]{:S(2)}) collective-permute-start(bf16[32,24,768]{2,1,0:T(8,128)(2,1)} %bitcast.33), channel_id=1, source_target_pairs={{0,1},{1,0},{2,3},{3,2},{4,5},{5,4},{6,7},{7,6},{8,9},{9,8},{10,11... | collective-permute-start | bytes 3538952 | tf_op jit(solution)/shard_map/ppermute | solution.py:762
  154.0 18.7 %collective-permute-start.19 = (bf16[1,24,6144]{2,1,0:T(8,128)(2,1)S(1)}, bf16[1,24,6144]{2,1,0:T(8,128)(2,1)S(1)}, u32[]{:S(2)}, u32[]{:S(2)}) collective-permute-start(bf16[1,24,6144]{2,1,0:T(8,128)(2,1)S(1)} %combine.11), channel_id=1, source_target_pairs={{0,16},{8,24},{16,0},{24,8},{1,17},{9,25},{17,1},{25,9},{2,18},{10... | collective-permute-start | bytes 884744 | tf_op jit(solution)/shard_map/ppermute | solution.py:553
  154.8 11.6 %collective-permute-start.15 = (bf16[8,24,768]{2,1,0:T(8,128)(2,1)S(1)}, bf16[8,24,768]{2,1,0:T(8,128)(2,1)S(1)}, u32[]{:S(2)}, u32[]{:S(2)}) collective-permute-start(bf16[8,24,768]{2,1,0:T(8,128)(2,1)S(1)} %get-tuple-element.138), channel_id=1, source_target_pairs={{0,2},{1,3},{2,0},{3,1},{4,6},{5,7},{6,4},{7,5},{8,10},{9,11},{10,... | collective-permute-start | bytes 884744 | tf_op jit(solution)/shard_map/ppermute | solution.py:553
  155.9 10.5 %collective-permute-start.16 = (bf16[8,24,768]{2,1,0:T(8,128)(2,1)S(1)}, bf16[8,24,768]{2,1,0:T(8,128)(2,1)S(1)}, u32[]{:S(2)}, u32[]{:S(2)}) collective-permute-start(bf16[8,24,768]{2,1,0:T(8,128)(2,1)S(1)} %get-tuple-element.139), channel_id=1, source_target_pairs={{0,4},{1,5},{2,6},{3,7},{4,0},{5,1},{6,2},{7,3},{8,12},{9,13},{10,... | collective-permute-start | bytes 884744 | tf_op jit(solution)/shard_map/ppermute | solution.py:553
  166.3 1.7 collective-permute-start.18
  168.6 9.1 %collective-permute-start.21 = (bf16[4,24,256]{2,1,0:T(8,128)(2,1)S(1)}, bf16[4,24,256]{2,1,0:T(8,128)(2,1)S(1)}, u32[]{:S(2)}, u32[]{:S(2)}) collective-permute-start(bf16[4,24,256]{2,1,0:T(8,128)(2,1)S(1)} %get-tuple-element.149), channel_id=1, source_target_pairs={{0,2},{1,3},{2,0},{3,1},{4,6},{5,7},{6,4},{7,5},{8,10},{9,11},{10,... | collective-permute-start | bytes 147464 | tf_op jit(solution)/shard_map/ppermute | solution.py:582
  169.2 8.5 %collective-permute-start.17 = (bf16[4,24,768]{2,1,0:T(8,128)(2,1)S(1)}, bf16[4,24,768]{2,1,0:T(8,128)(2,1)S(1)}, u32[]{:S(2)}, u32[]{:S(2)}) collective-permute-start(bf16[4,24,768]{2,1,0:T(8,128)(2,1)S(1)} %get-tuple-element.145), channel_id=1, source_target_pairs={{0,4},{1,5},{2,6},{3,7},{4,0},{5,1},{6,2},{7,3},{8,12},{9,13},{10,... | collective-permute-start | bytes 442376 | tf_op jit(solution)/shard_map/ppermute | solution.py:553
  171.0 6.7 %collective-permute-start.20 = (bf16[4,24,768]{2,1,0:T(8,128)(2,1)S(1)}, bf16[4,24,768]{2,1,0:T(8,128)(2,1)S(1)}, u32[]{:S(2)}, u32[]{:S(2)}) collective-permute-start(bf16[4,24,768]{2,1,0:T(8,128)(2,1)S(1)} %get-tuple-element.146), channel_id=1, source_target_pairs={{0,2},{1,3},{2,0},{3,1},{4,6},{5,7},{6,4},{7,5},{8,10},{9,11},{10,... | collective-permute-start | bytes 442376 | tf_op jit(solution)/shard_map/ppermute | solution.py:553
  172.0 5.2 %collective-permute-start.22 = (bf16[4,24,256]{2,1,0:T(8,128)(2,1)S(1)}, bf16[4,24,256]{2,1,0:T(8,128)(2,1)S(1)}, u32[]{:S(2)}, u32[]{:S(2)}) collective-permute-start(bf16[4,24,256]{2,1,0:T(8,128)(2,1)S(1)} %get-tuple-element.153), channel_id=1, source_target_pairs={{0,4},{1,5},{2,6},{3,7},{4,0},{5,1},{6,2},{7,3},{8,12},{9,13},{10,... | collective-permute-start | bytes 147464 | tf_op jit(solution)/shard_map/ppermute | solution.py:582
  172.7 5.0 %collective-permute-start.23 = (bf16[4,24,256]{2,1,0:T(8,128)(2,1)S(1)}, bf16[4,24,256]{2,1,0:T(8,128)(2,1)S(1)}, u32[]{:S(2)}, u32[]{:S(2)}) collective-permute-start(bf16[4,24,256]{2,1,0:T(8,128)(2,1)S(1)} %get-tuple-element.154), channel_id=1, source_target_pairs={{0,6},{1,7},{2,4},{3,5},{4,2},{5,3},{6,0},{7,1},{8,14},{9,15},{10,... | collective-permute-start | bytes 147464 | tf_op jit(solution)/shard_map/ppermute | solution.py:582
  178.5 4.6 %collective-permute-start.24 = (bf16[1,24,1792]{2,1,0:T(8,128)(2,1)S(1)}, bf16[1,24,1792]{2,1,0:T(8,128)(2,1)S(1)}, u32[]{:S(2)}, u32[]{:S(2)}) collective-permute-start(bf16[1,24,1792]{2,1,0:T(8,128)(2,1)S(1)} %get-tuple-element.155), channel_id=1, source_target_pairs={{0,8},{8,0},{16,24},{24,16},{1,9},{9,1},{17,25},{25,17},{2,10},{10... | collective-permute-start | bytes 258056 | tf_op jit(solution)/shard_map/ppermute | solution.py:582
  179.3 8.1 %collective-permute-start.25 = (bf16[1,24,1792]{2,1,0:T(8,128)(2,1)S(1)}, bf16[1,24,1792]{2,1,0:T(8,128)(2,1)S(1)}, u32[]{:S(2)}, u32[]{:S(2)}) collective-permute-start(bf16[1,24,1792]{2,1,0:T(8,128)(2,1)S(1)} %get-tuple-element.156), channel_id=1, source_target_pairs={{0,16},{8,24},{16,0},{24,8},{1,17},{9,25},{17,1},{25,9},{2,18},{10... | collective-permute-start | bytes 258056 | tf_op jit(solution)/shard_map/ppermute | solution.py:582
  182.2 6.3 %collective-permute-start.26 = (bf16[1,24,1792]{2,1,0:T(8,128)(2,1)S(1)}, bf16[1,24,1792]{2,1,0:T(8,128)(2,1)S(1)}, u32[]{:S(2)}, u32[]{:S(2)}) collective-permute-start(bf16[1,24,1792]{2,1,0:T(8,128)(2,1)S(1)} %get-tuple-element.157), channel_id=1, source_target_pairs={{0,24},{8,16},{16,8},{24,0},{1,25},{9,17},{17,9},{25,1},{2,26},{10... | collective-permute-start | bytes 258056 | tf_op jit(solution)/shard_map/ppermute | solution.py:582
  (9 other events, 28.2 us)
